TPU v7x, 32 devices: a whole 2x2x4 slice. The times are simulated.
32 devices in a mesh: replica: 8 (over z, y), tp: 4 (over x, core).
Axes of the slice: x: 2, y: 2, z: 4, core: 2. Of those that a mesh axis runs over, the one named last changes fastest.
Arguments:
- hidden: bfloat16 [96, 4, 8192], P('replica', None, 'tp'), may hold values from -6 to 6
- norm_gain: float32 [8192], replicated, may hold values from 0.5 to 1.5
- w_query: float32 [8192, 4096], P(('replica', 'tp')), may hold values from -0.0625 to 0.0625
- w_key: float32 [8192, 512], P(('replica', 'tp')), may hold values from -0.0625 to 0.0625
- w_value: float32 [8192, 512], P(('replica', 'tp')), may hold values from -0.0625 to 0.0625
- bias_query: float32 [4096], P('tp'), may hold values from -3 to 3
- bias_key: float32 [512], P('tp'), may hold values from -3 to 3
- bias_value: float32 [512], P('tp'), may hold values from -3 to 3
- key_pages: bfloat16 [512, 4, 128, 128], P(('replica', 'tp')), may hold values from -256 to 256
- value_pages: bfloat16 [512, 4, 128, 128], P(('replica', 'tp')), may hold values from -6 to 6
- kv_lengths: int32 [96], P(('replica', 'tp')), may hold values from 1 to 1024, as said below
- page_table: int32 [96, 8], P(('replica', 'tp')), may hold values from 0 to 15, as said below
Outputs:
- attended: bfloat16 [96, 4, 4096], P(('replica', 'tp'))
Inputs may be any that keep to these rules, and one draw needn't show every extreme that they name: `kv_lengths`: on every device, one row has exactly 1024 cached tokens. `page_table`: page ids are local to the pool of 16 pages of the device that holds the row. The first ceil(kv_lengths / 128) entries of a row name its pages in order; no page serves two of those entries on one device; later entries are arbitrary pages of the pool.
All inputs are finite; a program needn't handle non-finite values.
Results may differ from a plain program's by a relative error of at most 0.04.
Values may be sent and summed in bfloat16 or wider, within the bound.
No kernel may reach another device: no remote copies, remote signals or barrier semaphores. Data moves between devices by JAX's collectives and lax.ppermute only.
A program may use at most 128 MiB of HBM per device.

v0:
```python
import jax
import jax.numpy as jnp
from jax import lax
from jax.sharding import PartitionSpec as P

HD = 128
HQ = 32
KVH = 4
PAGE = 128
MOSTP = 8


EPS = 1e-06
THETA = 1000000.0


def rotate(values, positions):
    half = values.shape[-1] // 2
    freq = THETA ** (-(jnp.arange(half, dtype=jnp.float32) * 2.0 / values.shape[-1]))
    angle = positions.astype(jnp.float32)[..., None] * freq
    angle = jnp.concatenate([angle, angle], -1)[:, :, None, :]
    turned = jnp.concatenate([-values[..., half:], values[..., :half]], -1)
    return values * jnp.cos(angle) + turned * jnp.sin(angle)


def on_device(
    hidden,
    norm_gain,
    w_query,
    w_key,
    w_value,
    bias_query,
    bias_key,
    bias_value,
    key_pages,
    value_pages,
    kv_lengths,
    page_table,
):
    shards = (
        w_query.astype(jnp.bfloat16),
        w_key.astype(jnp.bfloat16),
        w_value.astype(jnp.bfloat16),
    )
    whole = lax.all_gather(hidden, "tp", axis=2, tiled=True)
    count, steps, width = whole.shape
    wide = whole.astype(jnp.float32)
    power = jnp.mean(wide * wide, axis=2, keepdims=True)
    normed = (
        (wide * lax.rsqrt(power + EPS) * norm_gain)
        .astype(jnp.bfloat16)
        .reshape(count * steps, width)
    )
    local = (
        lax.all_to_all(shards[0], "tp", split_axis=1, concat_axis=0, tiled=True),
        lax.all_to_all(shards[1], "tp", split_axis=1, concat_axis=0, tiled=True),
        lax.all_to_all(shards[2], "tp", split_axis=1, concat_axis=0, tiled=True),
    )
    pieces = (
        lax.all_gather(local[0], "replica", axis=0, tiled=True),
        lax.all_gather(local[1], "replica", axis=0, tiled=True),
        lax.all_gather(local[2], "replica", axis=0, tiled=True),
    )
    sums = tuple((jnp.dot(normed, piece, preferred_element_type=jnp.float32) for piece in pieces))
    made = [
        (total + bias).astype(jnp.bfloat16).reshape(count, steps, -1)
        for total, bias in zip(sums, (bias_query, bias_key, bias_value))
    ]
    query, key_new, value_new = (
        lax.all_to_all(made[0], "tp", split_axis=0, concat_axis=2, tiled=True),
        lax.all_to_all(made[1], "tp", split_axis=0, concat_axis=2, tiled=True),
        lax.all_to_all(made[2], "tp", split_axis=0, concat_axis=2, tiled=True),
    )
    rows = query.shape[0]
    steps = query.shape[1]
    query = query.reshape(rows, steps, HQ, HD)
    key_new = key_new.reshape(rows, steps, KVH, HD)
    value_new = value_new.reshape(rows, steps, KVH, HD)
    positions = kv_lengths[:, None] + jnp.arange(steps, dtype=jnp.int32)[None, :]
    query_rot = rotate(query.astype(jnp.float32), positions).astype(jnp.bfloat16)
    key_rot = rotate(key_new.astype(jnp.float32), positions).astype(jnp.bfloat16)
    group = HQ // KVH
    scale = 1.0 / HD**0.5
    q_heads = query_rot.reshape(rows, steps, KVH, group, HD)
    keys = jnp.take(key_pages, page_table, axis=0)
    vals = jnp.take(value_pages, page_table, axis=0)
    cache = (
        jnp.einsum("rtkgd,rmknd->rtkgmn", q_heads, keys, preferred_element_type=jnp.float32) * scale
    )
    spot = jnp.arange(MOSTP)[:, None] * PAGE + jnp.arange(PAGE)[None, :]
    live = (spot[None] < kv_lengths[:, None, None])[:, None, None, None]
    cache = jnp.where(live, cache, -1e30)
    causal = jnp.arange(steps)[None, :] <= jnp.arange(steps)[:, None]
    fresh = (
        jnp.einsum("rtkgd,rskd->rtkgs", q_heads, key_rot, preferred_element_type=jnp.float32)
        * scale
    )
    fresh = jnp.where(causal[None, :, None, None, :], fresh, -1e30)
    top = jnp.maximum(jnp.max(cache, axis=(4, 5)), jnp.max(fresh, axis=4))
    e_cache = jnp.where(live, jnp.exp(cache - top[..., None, None]), 0.0)
    e_fresh = jnp.where(causal[None, :, None, None, :], jnp.exp(fresh - top[..., None]), 0.0)
    total = jnp.sum(e_cache, axis=(4, 5)) + jnp.sum(e_fresh, axis=4)
    w_cache = (e_cache / total[..., None, None]).astype(jnp.bfloat16)
    w_fresh = (e_fresh / total[..., None]).astype(jnp.bfloat16)
    out = jnp.einsum("rtkgmn,rmknd->rtkgd", w_cache, vals, preferred_element_type=jnp.float32)
    out = out + jnp.einsum(
        "rtkgs,rskd->rtkgd", w_fresh, value_new, preferred_element_type=jnp.float32
    )
    return out.reshape(rows, steps, HQ * HD).astype(jnp.bfloat16)


def solution(mesh):
    in_specs = (
        P("replica", None, "tp"),
        P(),
        P(("replica", "tp"), None),
        P(("replica", "tp"), None),
        P(("replica", "tp"), None),
        P("tp"),
        P("tp"),
        P("tp"),
        P(("replica", "tp"), None, None, None),
        P(("replica", "tp"), None, None, None),
        P(("replica", "tp")),
        P(("replica", "tp"), None),
    )
    out_specs = P(("replica", "tp"), None, None)
    return jax.shard_map(
        on_device, mesh=mesh, in_specs=in_specs, out_specs=out_specs, check_vma=False
    )
```

profile of v0, /device:TPU:0, one launch (start us, length us, event | category | flops | bytes accessed | tf_op | source)
XLA Modules:
  0.0 380.4 jit_solution(5661806267189946849)
XLA Ops:
  6.5 1.3 copy.32
  7.9 10.0 %all_to_all.90 = bf16[256,4,128]{0,2,1:T(8,128)(2,1)S(1)} all-to-all(bf16[256,4,128]{0,2,1:T(8,128)(2,1)S(1)} %bitcast.101), channel_id=1, replica_groups=mesh['replica'=8,'tp'=4] {'tp'}, dimensions={1} | all-to-all | bytes 524288 | tf_op jit(solution)/shard_map/all_to_all | solution.py:56
  17.9 0.8 copy.33
  18.8 0.0 all-gather.6.cloned.1.call-update
  18.8 0.0 all-gather.8.cloned.1.call-start
  18.8 0.1 copy.37
  19.0 8.4 %all_to_all.91 = bf16[256,4,128]{0,2,1:T(8,128)(2,1)S(1)} all-to-all(bf16[256,4,128]{0,2,1:T(8,128)(2,1)S(1)} %bitcast.102), channel_id=1, replica_groups=mesh['replica'=8,'tp'=4] {'tp'}, dimensions={1} | all-to-all | bytes 524288 | tf_op jit(solution)/shard_map/all_to_all | solution.py:57
  27.4 0.9 copy.38
  28.3 0.0 all-gather.4.cloned.1.call-start
  28.3 4.6 %copy.27 = bf16[256,4096]{0,1:T(8,128)(2,1)} copy(f32[256,4096]{1,0:T(8,128)} %param.16) | data formatting | bytes 6291456 | tf_op args[2]
  32.9 30.1 %all_to_all.92 = bf16[256,4,1024]{0,2,1:T(8,128)(2,1)} all-to-all(bf16[256,4,1024]{0,2,1:T(8,128)(2,1)} %bitcast.96), channel_id=1, replica_groups=mesh['replica'=8,'tp'=4] {'tp'}, dimensions={1} | all-to-all | bytes 4194304 | tf_op jit(solution)/shard_map/all_to_all | solution.py:55
  63.1 4.0 %copy.28 = bf16[4,256,1024]{2,1,0:T(8,128)(2,1)} copy(bf16[4,256,1024]{1,2,0:T(8,128)(2,1)} %bitcast.98) | data formatting | bytes 4194304 | tf_op jit(solution)/shard_map/all_to_all | solution.py:55
  67.1 0.9 copy-done.3
  68.0 7.8 %all_gather.12 = bf16[12,4,8192]{2,1,0:T(4,128)(2,1)S(1)} all-gather(bf16[12,4,2048]{2,1,0:T(4,128)(2,1)S(1)} %copy-done.3), channel_id=1, replica_groups=mesh['replica'=8,'tp'=4] {'tp'}, dimensions={2}, use_global_device_ids=true | all-gather | bytes 983040 | tf_op jit(solution)/shard_map/all_gather | solution.py:45
  75.8 0.5 fusion.6
  76.3 1.4 fusion.8
  77.7 1.6 reshape.170
  79.3 0.1 reshape.199
  79.4 2.7 gather_fusion.1
  82.2 4.3 %gather_fusion = bf16[24,4,128,128]{3,2,1,0:T(8,128)(2,1)} fusion(bf16[16,4,128,128]{3,2,1,0:T(8,128)(2,1)} %param.23, s32[1024]{0:T(1024)S(1)} %pad_clamp_fusion), kind=kCustom, calls=%fused_computation.clone | custom fusion | bytes 6291552 | tf_op jit(solution)/shard_map/jit(_take)/gather | solution.py:86
  86.5 0.1 add_convert_fusion
  86.6 0.1 broadcast_multiply_fusion
  86.7 0.1 fusion.47
  86.8 0.1 iota_add_fusion
  86.9 0.1 broadcast_compare_fusion
  87.0 2.7 fusion.24
  89.6 3.4 all-to-all-start.3
  93.0 25.1 %all-gather.8.cloned.1.call-done = bf16[8192,128]{1,0:T(8,128)(2,1)} async-done(((bf16[1024,128]{1,0:T(8,128)(2,1)}), bf16[8192,128]{1,0:T(8,128)(2,1)}) %all-gather.8.cloned.1.call-update) | async-done | bytes 2097168 | tf_op jit(solution)/shard_map/all_gather | solution.py:62
  118.2 2.7 fusion.25
  120.8 225.3 %all-gather.4.cloned.1.call-done = bf16[8192,1024]{1,0:T(8,128)(2,1)} async-done(((bf16[1024,1024]{1,0:T(8,128)(2,1)}), bf16[8192,1024]{1,0:T(8,128)(2,1)}) %all-gather.4.cloned.1.call-update) | async-done | bytes 16777232 | tf_op jit(solution)/shard_map/all_gather | solution.py:60
  346.1 8.8 %fusion.19 = bf16[48,1024]{1,0:T(8,128)(2,1)S(1)} fusion(bf16[48,8192]{1,0:T(8,128)(2,1)S(1)} %reshape.170, bf16[8192,1024]{1,0:T(8,128)(2,1)} %all-gather.4.cloned.1.call-done, f32[1024]{0:T(1024)S(1)} %copy-done.6), kind=kOutput, calls=%fused_computation.27 | convolution fusion | flops 805404672 | bytes 17666048 | tf_op jit(solution)/shard_map/dot_general | solution.py:64
  354.9 0.7 reshape.171
  355.6 3.3 all-to-all-start.1
  358.9 0.1 slice_negate_fusion.1
  359.0 4.2 %all-to-all-done.1 = bf16[12,4,1024]{2,1,0:T(4,128)(2,1)S(1)} async-done(((bf16[12,4,1024]{2,1,0:T(4,128)(2,1)}), bf16[12,4,1024]{2,1,0:T(4,128)(2,1)S(1)}, u32[]{:S(2)}, u32[]{:S(2)}) %all-to-all-start.1) | async-done | bytes 98336 | tf_op jit(solution)/shard_map/all_to_all | solution.py:70
  363.2 3.4 all-to-all-start.5
  366.6 0.1 copy.30
  366.8 0.1 reshape.174
  366.9 0.1 reshape.175
  367.0 0.1 fusion.30
  367.1 0.1 fusion.32
  367.2 0.6 fusion.52
  367.8 3.4 bitcast_reduce_fusion
  371.2 0.2 fusion.35
  371.4 0.4 fusion.15
  371.8 1.0 fusion.16
  372.8 0.3 fusion.21
  373.2 0.7 convert_element_type.107
  (37 shorter events, 0.2 us)
Async XLA Ops:
  6.5 72.9 %copy-start = (bf16[16,4,128,128]{3,2,1,0:T(8,128)(2,1)S(1)}, bf16[16,4,128,128]{3,2,1,0:T(8,128)(2,1)}, u32[]{:S(2)}) copy-start(bf16[16,4,128,128]{3,2,1,0:T(8,128)(2,1)} %param.22) | copy-start | bytes 6291460
  6.5 12.3 %copy-start.2 = (f32[256,512]{1,0:T(8,128)S(1)}, f32[256,512]{1,0:T(8,128)}, u32[]{:S(2)}) copy-start(f32[256,512]{1,0:T(8,128)} %param.18) | copy-start | bytes 1572868
  6.5 80.4 %all-gather.6.cloned.1.call-start = ((), (), s32[]{:S(2)}) async-start(), calls=%async_computation.7 | async-start | bytes 2359296 | tf_op jit(solution)/shard_map/all_gather | solution.py:61
  18.8 99.4 %all-gather.8.cloned.1.call-start = ((), (), s32[]{:S(2)}) async-start(), calls=%async_computation.8 | async-start | bytes 2359296 | tf_op jit(solution)/shard_map/all_gather | solution.py:62
  28.3 317.9 %all-gather.4.cloned.1.call-start = ((), (), s32[]{:S(2)}) async-start(), calls=%async_computation.6 | async-start | bytes 18874368 | tf_op jit(solution)/shard_map/all_gather | solution.py:60
  67.0 0.9 copy-start.3
  67.0 9.3 %copy-start.4 = (f32[8192]{0:T(1024)S(1)}, f32[8192]{0:T(1024)}, u32[]{:S(2)}) copy-start(f32[8192]{0:T(1024)} %param.15) | copy-start | bytes 98308
  75.8 3.5 copy-start.5
  82.2 4.4 %copy-start.7 = (s32[3]{0:T(128)S(1)}, s32[3]{0:T(128)}, u32[]{:S(2)}) copy-start(s32[3]{0:T(128)} %param.24) | copy-start | bytes 40
  82.2 4.8 %copy-start.8 = (f32[128]{0:T(128)S(1)}, f32[128]{0:T(128)}, u32[]{:S(2)}) copy-start(f32[128]{0:T(128)} %param.20) | copy-start | bytes 1540
  86.5 31.7 %copy-start.9 = (f32[128]{0:T(128)S(1)}, f32[128]{0:T(128)}, u32[]{:S(2)}) copy-start(f32[128]{0:T(128)} %param.21) | copy-start | bytes 1540
  89.6 256.5 %copy-start.6 = (f32[1024]{0:T(1024)S(1)}, f32[1024]{0:T(1024)}, u32[]{:S(2)}) copy-start(f32[1024]{0:T(1024)} %param.19) | copy-start | bytes 12292
  89.6 31.2 %all-to-all-start.3 = ((bf16[12,4,128]{2,1,0:T(4,128)(2,1)}), bf16[12,4,128]{2,1,0:T(4,128)(2,1)S(1)}, u32[]{:S(2)}, u32[]{:S(2)}) async-start(bf16[12,4,128]{2,1,0:T(4,128)(2,1)} %bitcast.19), calls=%async_computation.3 | async-start | bytes 24576 | tf_op jit(solution)/shard_map/all_to_all | solution.py:71
  355.6 7.6 %all-to-all-start.1 = ((bf16[12,4,1024]{2,1,0:T(4,128)(2,1)}), bf16[12,4,1024]{2,1,0:T(4,128)(2,1)S(1)}, u32[]{:S(2)}, u32[]{:S(2)}) async-start(bf16[12,4,1024]{2,1,0:T(4,128)(2,1)} %reshape.171), calls=%async_computation.1 | async-start | bytes 196608 | tf_op jit(solution)/shard_map/all_to_all | solution.py:70
  363.2 9.6 %all-to-all-start.5 = ((bf16[12,4,128]{2,1,0:T(4,128)(2,1)}), bf16[12,4,128]{2,1,0:T(4,128)(2,1)S(1)}, u32[]{:S(2)}, u32[]{:S(2)}) async-start(bf16[12,4,128]{2,1,0:T(4,128)(2,1)} %bitcast.30), calls=%async_computation.5 | async-start | bytes 24576 | tf_op jit(solution)/shard_map/all_to_all | solution.py:72
  367.8 4.0 %copy-start.1 = (bf16[24,4,128,128]{3,2,1,0:T(8,128)(2,1)S(1)}, bf16[24,4,128,128]{3,2,1,0:T(8,128)(2,1)}, u32[]{:S(2)}) copy-start(bf16[24,4,128,128]{3,2,1,0:T(8,128)(2,1)} %gather_fusion) | copy-start | bytes 9437188
Sparse Core Ops, SparseCore 0:
  18.9 49.3 all-gather.5
  70.5 47.6 all-gather.7
  120.3 225.7 all-gather.3
where the time goes:
time: 381 us; the launch traced here: 380 us
  waiting for transfers between devices  255 us (67%)
  blocking collectives  56.4 us (15%)
  local copies, waits for them, and re-layouts  23.1 us (6%)
  matrix products  19.4 us (5%)
  between operations  13.4 us (4%)
  starting transfers between devices  10.2 us (3%)
    all_gather x1, waiting for transfers between devices, on_device(): lax.all_gather(local[0], 'replica', axis=0, tiled=True)  225 us
    all_to_all x1, blocking collectives, on_device(): lax.all_to_all(shards[0], 'tp', split_axis=1, concat_axis=0, tiled=True)  30.1 us
    all_gather x1, waiting for transfers between devices, on_device(): lax.all_gather(local[2], 'replica', axis=0, tiled=True)  25.1 us
    dot_general x3, matrix products, on_device(): jnp.dot(normed, piece, preferred_element_type=jnp.float32)  14.1 us
    all_to_all x1, blocking collectives, on_device(): lax.all_to_all(shards[1], 'tp', split_axis=1, concat_axis=0, tiled=True)  10 us
    all_to_all x1, blocking collectives, on_device(): lax.all_to_all(shards[2], 'tp', split_axis=1, concat_axis=0, tiled=True)  8.39 us
    all_gather x1, blocking collectives, on_device(): whole = lax.all_gather(hidden, 'tp', axis=2, tiled=True)  7.81 us
  transfers between devices with their start and end apart: 6, of which 3 were waited for; matrix products, arithmetic and copies ran while one was open for 8% of the time, Pallas kernels for 0%

commit v1 on v0

v1 whole, which is shorter than its diff:
```python
import jax
import jax.numpy as jnp
from jax import lax
from jax.sharding import PartitionSpec as P

HD = 128
HQ = 32
KVH = 4
PAGE = 128
MOSTP = 8
EPS = 1e-06
THETA = 1000000.0
AXES = ("replica", "tp")
BF = jnp.bfloat16
F32 = jnp.float32


def rotate(values, positions):
    half = values.shape[-1] // 2
    freq = THETA ** (-(jnp.arange(half, dtype=jnp.float32) * 2.0 / values.shape[-1]))
    angle = positions.astype(jnp.float32)[..., None] * freq
    angle = jnp.concatenate([angle, angle], -1)[:, :, None, :]
    turned = jnp.concatenate([-values[..., half:], values[..., :half]], -1)
    return values * jnp.cos(angle) + turned * jnp.sin(angle)


def attend(query, key_new, value_new, key_pages, value_pages, kv_lengths, page_table):
    rows, steps = query.shape[:2]
    positions = kv_lengths[:, None] + jnp.arange(steps, dtype=jnp.int32)[None, :]
    query_rot = rotate(query.astype(jnp.float32), positions).astype(jnp.bfloat16)
    key_rot = rotate(key_new.astype(jnp.float32), positions).astype(jnp.bfloat16)
    group = HQ // KVH
    scale = 1.0 / HD**0.5
    q_heads = query_rot.reshape(rows, steps, KVH, group, HD)
    keys = jnp.take(key_pages, page_table, axis=0)
    vals = jnp.take(value_pages, page_table, axis=0)
    cache = (
        jnp.einsum("rtkgd,rmknd->rtkgmn", q_heads, keys, preferred_element_type=jnp.float32) * scale
    )
    spot = jnp.arange(MOSTP)[:, None] * PAGE + jnp.arange(PAGE)[None, :]
    live = (spot[None] < kv_lengths[:, None, None])[:, None, None, None]
    cache = jnp.where(live, cache, -1e30)
    causal = jnp.arange(steps)[None, :] <= jnp.arange(steps)[:, None]
    fresh = (
        jnp.einsum("rtkgd,rskd->rtkgs", q_heads, key_rot, preferred_element_type=jnp.float32)
        * scale
    )
    fresh = jnp.where(causal[None, :, None, None, :], fresh, -1e30)
    top = jnp.maximum(jnp.max(cache, axis=(4, 5)), jnp.max(fresh, axis=4))
    e_cache = jnp.where(live, jnp.exp(cache - top[..., None, None]), 0.0)
    e_fresh = jnp.where(causal[None, :, None, None, :], jnp.exp(fresh - top[..., None]), 0.0)
    total = jnp.sum(e_cache, axis=(4, 5)) + jnp.sum(e_fresh, axis=4)
    w_cache = (e_cache / total[..., None, None]).astype(jnp.bfloat16)
    w_fresh = (e_fresh / total[..., None]).astype(jnp.bfloat16)
    out = jnp.einsum("rtkgmn,rmknd->rtkgd", w_cache, vals, preferred_element_type=jnp.float32)
    out = out + jnp.einsum(
        "rtkgs,rskd->rtkgd", w_fresh, value_new, preferred_element_type=jnp.float32
    )
    return out.reshape(rows, steps, HQ * HD).astype(jnp.bfloat16)


def weights_plan(hidden, norm_gain, w_query, w_key, w_value, bias_query, bias_key, bias_value,
                 key_pages, value_pages, kv_lengths, page_table):
    shards = tuple(w.astype(BF) for w in (w_query, w_key, w_value))
    whole = lax.all_gather(hidden, "tp", axis=2, tiled=True)
    count, steps, width = whole.shape
    wide = whole.astype(F32)
    power = jnp.mean(wide * wide, axis=2, keepdims=True)
    normed = (wide * lax.rsqrt(power + EPS) * norm_gain).astype(BF).reshape(count * steps, width)
    made = []
    for shard, bias in zip(shards, (bias_query, bias_key, bias_value)):
        local = lax.all_to_all(shard, "tp", split_axis=1, concat_axis=0, tiled=True)
        piece = lax.all_gather(local, "replica", axis=0, tiled=True)
        total = jnp.dot(normed, piece, preferred_element_type=F32) + bias
        out = total.astype(BF).reshape(count, steps, -1)
        made.append(lax.all_to_all(out, "tp", split_axis=0, concat_axis=2, tiled=True))
    rows = made[0].shape[0]
    query = made[0].reshape(rows, steps, HQ, HD)
    key_new = made[1].reshape(rows, steps, KVH, HD)
    value_new = made[2].reshape(rows, steps, KVH, HD)
    return attend(query, key_new, value_new, key_pages, value_pages, kv_lengths, page_table)


def sums_plan(R, T, hidden, norm_gain, w_query, w_key, w_value, bias_query, bias_key, bias_value,
              key_pages, value_pages, kv_lengths, page_table):
    ri, ti = lax.axis_index("replica"), lax.axis_index("tp")
    me = ri * T + ti
    y, z, c, x = ri % 2, ri // 2, ti % 2, ti // 2
    Z = R // 2
    count, steps, _ = hidden.shape
    kw = w_query.shape[0]
    D = norm_gain.shape[0]
    rows = count // T
    own = rows * steps
    G = KVH // 2
    qw = HQ // KVH * HD
    gw = qw + 2 * HD

    def perm(f):
        pairs = []
        for i in range(R * T):
            r, t = divmod(i, T)
            zz, yy, xx, cc = f(r // 2, r % 2, t // 2, t % 2)
            pairs.append((i, (zz * 2 + yy) * T + xx * 2 + cc))
        return pairs

    to_core = perm(lambda z, y, x, c: (z, y, x, 1 - c))
    to_x = perm(lambda z, y, x, c: (z, y, 1 - x, c))
    to_y = perm(lambda z, y, x, c: (z, 1 - y, x, c))

    def send(a, pairs):
        return lax.ppermute(a, AXES, pairs)

    pick = lambda a, i, axis=0: lax.dynamic_index_in_dim(a, i, axis, keepdims=False)

    got = []
    for k in range(R):
        part = lax.dynamic_slice_in_dim(hidden, (ri ^ k) * kw, kw, 2)
        pairs = [(r * T + t, t * R + (r ^ k)) for r in range(R) for t in range(T)]
        got.append(send(part, pairs))
    j = me % R
    acts = jnp.take(jnp.stack(got), j ^ jnp.arange(R), axis=0)
    acts = acts.reshape(Z, 2, 2, 2 * own, kw).transpose(1, 2, 0, 3, 4).reshape(2, 2, Z * 2 * own, kw)
    acts_sib = send(acts, to_core)

    gain = lax.dynamic_slice_in_dim(norm_gain, me * kw, kw)[:, None]

    def columns(cc, g):
        h = cc + 2 * g
        parts = [
            lax.dynamic_slice_in_dim(w_query, h * qw, qw, 1),
            lax.dynamic_slice_in_dim(w_key, h * HD, HD, 1),
            lax.dynamic_slice_in_dim(w_value, h * HD, HD, 1),
        ]
        return (jnp.concatenate(parts, 1) * gain).astype(BF)

    w_own = [columns(c, g) for g in range(G)]
    w_sib = [send(columns(1 - c, g), to_core) for g in range(G)]

    wide = hidden.astype(F32)
    power = jnp.sum(wide * wide, axis=2).reshape(T, own)
    bias = jnp.concatenate([bias_query, bias_key, bias_value])
    biases = [bias]
    squares = pick(power, ti)
    for k in range(1, T):
        msg = jnp.concatenate([bias, pick(power, ti ^ k)])
        pairs = [(r * T + t, r * T + (t ^ k)) for r in range(R) for t in range(T)]
        msg = send(msg, pairs)
        biases.append(msg[: bias.shape[0]])
        squares = squares + msg[bias.shape[0] :]
    bias_all = jnp.take(jnp.stack(biases), ti ^ jnp.arange(T), axis=0)
    row_scale = lax.rsqrt(squares / D + EPS)

    def dot(g):
        f = lambda a, w: jnp.einsum("yxmk,kn->yxmn", a, w, preferred_element_type=F32)
        return f(acts, w_own[g]) + f(acts_sib, w_sib[g])

    done = []
    for g in range(G):
        part = dot(g)
        first, second = ((x, 1, to_x), (y, 0, to_y)) if g % 2 == 0 else ((y, 0, to_y), (x, 0, to_x))
        i, axis, pairs = first
        part = pick(part, i, axis) + send(pick(part, 1 - i, axis).astype(BF), pairs).astype(F32)
        i, axis, pairs = second
        part = pick(part, i, axis) + send(pick(part, 1 - i, axis).astype(BF), pairs).astype(F32)
        part = part.reshape(Z, 2 * own, gw)
        total = pick(part, z)
        for k in range(1, Z):
            pairs = perm(lambda z, y, x, c: (z ^ k, y, x, c))
            total = total + send(pick(part, z ^ k).astype(BF), pairs).astype(F32)
        done.append(total.reshape(2, own, gw))
    done = jnp.stack(done)
    mine = pick(done, c, 1)
    other = send(pick(done, 1 - c, 1), to_core)
    low, high = jnp.where(c == 0, mine, other), jnp.where(c == 0, other, mine)
    full = jnp.stack([low, high], 1).reshape(KVH, own, gw)
    full = full * row_scale[None, :, None] + bias_all[:, None, :]
    full = full.astype(BF).reshape(KVH, rows, steps, gw)
    query = full[..., :qw].reshape(KVH, rows, steps, HQ // KVH, HD).transpose(1, 2, 0, 3, 4)
    query = query.reshape(rows, steps, HQ, HD)
    key_new = full[..., qw : qw + HD].transpose(1, 2, 0, 3)
    value_new = full[..., qw + HD :].transpose(1, 2, 0, 3)
    return attend(query, key_new, value_new, key_pages, value_pages, kv_lengths, page_table)


def solution(mesh):
    R, T = mesh.shape["replica"], mesh.shape["tp"]

    def on_device(hidden, norm_gain, *rest):
        m = hidden.shape[0] * hidden.shape[1] * R
        few_rows = m * T < norm_gain.shape[0]
        two_ways = T == KVH and R & (R - 1) == 0 and R > T
        if few_rows and two_ways:
            return sums_plan(R, T, hidden, norm_gain, *rest)
        return weights_plan(hidden, norm_gain, *rest)

    split = ("replica", "tp")
    in_specs = (
        P("replica", None, "tp"), P(), P(split, None), P(split, None), P(split, None),
        P("tp"), P("tp"), P("tp"),
        P(split, None, None, None), P(split, None, None, None), P(split), P(split, None),
    )
    return jax.shard_map(
        on_device, mesh=mesh, in_specs=in_specs, out_specs=P(split, None, None), check_vma=False
    )
```

time: 381 us -> 108 us (0.28)
  waiting for transfers between devices: 255 us -> 27.3 us
  blocking collectives: 56.4 us -> 0 us
  starting transfers between devices: 10.2 us -> 38.5 us
  between operations: 13.4 us -> 0.81 us
  matrix products: 19.4 us -> 10.7 us
  other arithmetic: 3.37 us -> 8.91 us
    all_gather x3 -> x0, waiting for transfers between devices: 250 us -> none  [the longest x1 225 us: on_device(): lax.all_gather(local[0], 'replica', axis=0, tiled=True)]
    all_to_all x3 -> x0, blocking collectives: 48.5 us -> none  [the longest x1 30.1 us: on_device(): lax.all_to_all(shards[0], 'tp', split_axis=1, concat_axis=0, tiled=True)]
    ppermute x0 -> x25, starting transfers between devices: none -> 38.5 us  [send(): return lax.ppermute(a, AXES, pairs)]
    ppermute x0 -> x25, waiting for transfers between devices: none -> 27.3 us  [send(): return lax.ppermute(a, AXES, pairs)]
    all_to_all x3 -> x0, starting transfers between devices: 10.1 us -> none  [the longest x1 3.41 us: on_device(): lax.all_to_all(made[2], 'tp', split_axis=0, concat_axis=2, tiled=True)]
    dot_general x7 -> x8, matrix products: 19.4 us -> 10.7 us  [the longest x4 5.44 us: dot(): jnp.einsum('yxmk,kn->yxmn', a, w, preferred_element_type=F32)]
    all_gather x1 -> x0, blocking collectives: 7.81 us -> none  [on_device(): whole = lax.all_gather(hidden, 'tp', axis=2, tiled=True)]
    dynamic_slice x0 -> x7, local copies, waits for them, and re-layouts: none -> 6.38 us  [the longest x1 3.69 us: columns(): lax.dynamic_slice_in_dim(w_query, h * qw, qw, 1)]
  transfers between devices with their start and end apart: 6 -> 25, of which waited for: 3 -> 8; matrix products, arithmetic and copies ran while one was open for 8% -> 23% of each run, Pallas kernels for 0% -> 0%
where the time goes in v1:
time: 108 us
  starting transfers between devices  38.5 us (36%)
  waiting for transfers between devices  27.3 us (25%)
  local copies, waits for them, and re-layouts  21.4 us (20%)
  matrix products  10.7 us (10%)
  other arithmetic  8.91 us (8%)
    ppermute x25, starting transfers between devices, send(): return lax.ppermute(a, AXES, pairs)  38.5 us
    ppermute x25, waiting for transfers between devices, send(): return lax.ppermute(a, AXES, pairs)  27.3 us
    dot_general x4, matrix products, dot(): jnp.einsum('yxmk,kn->yxmn', a, w, preferred_element_type=F32)  5.44 us
    gather x1, local copies, waits for them, and re-layouts, attend(): vals = jnp.take(value_pages, page_table, axis=0)  4.29 us
    dynamic_slice x1, local copies, waits for them, and re-layouts, columns(): lax.dynamic_slice_in_dim(w_query, h * qw, qw, 1)  3.69 us
    dot_general x1, matrix products, attend(): jnp.einsum('rtkgd,rmknd->rtkgmn', q_heads, keys, preferred_element_type=j...  3.35 us
    gather x1, local copies, waits for them, and re-layouts, attend(): keys = jnp.take(key_pages, page_table, axis=0)  2.73 us
  transfers between devices with their start and end apart: 25, of which 8 were waited for; matrix products, arithmetic and copies ran while one was open for 23% of the time, Pallas kernels for 0%

profile of v1, /device:TPU:0, one launch (start us, length us, event | category | flops | bytes accessed | tf_op | source)
XLA Modules:
  0.0 107.6 jit_solution(1639485906111444869)
XLA Ops:
  0.0 0.9 dynamic_slice.146
  0.9 3.7 %constant_dynamic-slice_fusion.8 = (f32[256,1024]{1,0:T(8,128)S(1)}, f32[256,1024]{1,0:T(8,128)S(1)}, f32[256,1024]{1,0:T(8,128)S(1)}, f32[256,1024]{1,0:T(8,128)}) fusion(f32[256,4096]{1,0:T(8,128)} %param.16, s32[]{:T(128)S(6)} %select_n.247, s32[]{:T(128)S(6)} %select_n.232, s32[]{:T(128)S(6)} %select_n.229, s32[]{:T(128)S(6)} %select_n.245), kind=kLoop, calls=%fused_computation.135 | loop fusion | bytes 8388624 | tf_op jit(solution)/shard_map/dynamic_slice | solution.py:131
  4.6 0.9 constant_dynamic-slice_fusion.6
  5.6 1.4 %fusion.15 = (bf16[256,1280]{1,0:T(8,128)(2,1)}, bf16[256,1280]{1,0:T(8,128)(2,1)}) fusion(f32[256,128]{1,0:T(8,128)S(1)} %get-tuple-element.14, f32[256,128]{1,0:T(8,128)S(1)} %get-tuple-element.58, f32[256,1024]{1,0:T(8,128)S(1)} %get-tuple-element.6, f32[256]{0:T(256)S(1)} %dynamic_slice.146, f32[256,128]{1,0:T(8,128)S(1)} %get-tuple-element.15, ...), kind=kLoop, calls=%fused_computation.29 | loop fusion | flops 2621440 | bytes 3933184 | tf_op jit(solution)/shard_map/convert_element_type | solution.py:135
  7.4 0.7 constant_dynamic-slice_fusion.18
  8.1 0.7 collective-permute-start
  9.2 4.0 %collective-permute-start.22 = (f32[1292]{0:T(1024)S(1)}, f32[1292]{0:T(1024)S(1)}, u32[]{:S(2)}, u32[]{:S(2)}) collective-permute-start(f32[1292]{0:T(1024)S(1)} %get-tuple-element.42), channel_id=1, source_target_pairs={{0,1},{1,0},{2,3},{3,2},{4,5},{5,4},{6,7},{7,6},{8,9},{9,8},{10,11... | collective-permute-start | bytes 15512 | tf_op jit(solution)/shard_map/ppermute | solution.py:112
  13.1 3.5 %collective-permute-start.23 = (f32[1292]{0:T(1024)S(1)}, f32[1292]{0:T(1024)S(1)}, u32[]{:S(2)}, u32[]{:S(2)}) collective-permute-start(f32[1292]{0:T(1024)S(1)} %get-tuple-element.43), channel_id=1, source_target_pairs={{0,2},{1,3},{2,0},{3,1},{4,6},{5,7},{6,4},{7,5},{8,10},{9,11},{10,... | collective-permute-start | bytes 15512 | tf_op jit(solution)/shard_map/ppermute | solution.py:112
  16.6 0.6 compare_and_fusion.2
  17.3 0.6 compare_and_fusion
  17.9 0.6 pad_clamp_fusion.1
  18.9 0.7 broadcast_compare_fusion
  20.2 0.7 squeeze.60
  20.8 2.7 %gather_fusion.3 = bf16[24,4,128,128]{3,2,1,0:T(8,128)(2,1)} fusion(bf16[16,4,128,128]{3,2,1,0:T(8,128)(2,1)S(1)} %copy-done, s32[1024]{0:T(1024)S(1)} %pad_clamp_fusion.2), kind=kCustom, calls=%fused_computation.1.clone | custom fusion | bytes 6291552 | tf_op jit(solution)/shard_map/jit(_take)/gather | solution.py:35
  23.6 4.3 %gather_fusion.2 = bf16[24,4,128,128]{3,2,1,0:T(8,128)(2,1)} fusion(bf16[16,4,128,128]{3,2,1,0:T(8,128)(2,1)} %param.23, s32[1024]{0:T(1024)S(1)} %pad_clamp_fusion.2), kind=kCustom, calls=%fused_computation.clone | custom fusion | bytes 6291552 | tf_op jit(solution)/shard_map/jit(_take)/gather | solution.py:36
  28.0 2.6 %collective-permute-start.2 = (bf16[12,4,256]{2,1,0:T(4,128)(2,1)}, bf16[12,4,256]{2,1,0:T(4,128)(2,1)S(1)}, u32[]{:S(2)}, u32[]{:S(2)}) collective-permute-start(bf16[12,4,256]{2,1,0:T(4,128)(2,1)} %get-tuple-element.35), channel_id=1, source_target_pairs={{0,2},{1,10},{2,18},{3,26},{4,3},{5,11},{6,19},{7,27},{8,0},{9,8},... | collective-permute-start | bytes 73736 | tf_op jit(solution)/shard_map/ppermute | solution.py:112
  30.7 3.8 %collective-permute-start.3 = (bf16[12,4,256]{2,1,0:T(4,128)(2,1)}, bf16[12,4,256]{2,1,0:T(4,128)(2,1)S(1)}, u32[]{:S(2)}, u32[]{:S(2)}) collective-permute-start(bf16[12,4,256]{2,1,0:T(4,128)(2,1)} %get-tuple-element.34), channel_id=1, source_target_pairs={{0,3},{1,11},{2,19},{3,27},{4,2},{5,10},{6,18},{7,26},{8,1},{9,9},... | collective-permute-start | bytes 73736 | tf_op jit(solution)/shard_map/ppermute | solution.py:112
  35.0 0.7 broadcast_select_fusion
  35.7 0.7 slice.64
  36.4 0.7 slice.66
  37.1 0.7 slice.68
  37.7 0.6 copy-done.11
  38.4 0.6 collective-permute-start.4
  39.0 0.7 bitcast_dynamic-update-slice_fusion.7
  39.7 3.1 %collective-permute-start.5 = (bf16[12,4,256]{2,1,0:T(4,128)(2,1)S(1)}, bf16[12,4,256]{2,1,0:T(4,128)(2,1)S(1)}, u32[]{:S(2)}, u32[]{:S(2)}) collective-permute-start(bf16[12,4,256]{2,1,0:T(4,128)(2,1)S(1)} %copy-done.10), channel_id=1, source_target_pairs={{0,5},{1,13},{2,21},{3,29},{4,4},{5,12},{6,20},{7,28},{8,7},{9,15}... | collective-permute-start | bytes 73736 | tf_op jit(solution)/shard_map/ppermute | solution.py:112
  42.8 7.8 %collective-permute-start.6 = (bf16[12,4,256]{2,1,0:T(4,128)(2,1)S(1)}, bf16[12,4,256]{2,1,0:T(4,128)(2,1)S(1)}, u32[]{:S(2)}, u32[]{:S(2)}) collective-permute-start(bf16[12,4,256]{2,1,0:T(4,128)(2,1)S(1)} %copy-done.9), channel_id=1, source_target_pairs={{0,6},{1,14},{2,22},{3,30},{4,7},{5,15},{6,23},{7,31},{8,4},{9,12}... | collective-permute-start | bytes 73736 | tf_op jit(solution)/shard_map/ppermute | solution.py:112
  51.2 1.9 %collective-permute-done.6 = bf16[12,4,256]{2,1,0:T(4,128)(2,1)S(1)} collective-permute-done((bf16[12,4,256]{2,1,0:T(4,128)(2,1)S(1)}, bf16[12,4,256]{2,1,0:T(4,128)(2,1)S(1)}, u32[]{:S(2)}, u32[]{:S(2)}) %collective-permute-start.6) | collective-permute-done | bytes 24608 | tf_op jit(solution)/shard_map/ppermute | solution.py:112
  53.1 4.2 %collective-permute-done.7 = bf16[12,4,256]{2,1,0:T(4,128)(2,1)S(1)} collective-permute-done((bf16[12,4,256]{2,1,0:T(4,128)(2,1)S(1)}, bf16[12,4,256]{2,1,0:T(4,128)(2,1)S(1)}, u32[]{:S(2)}, u32[]{:S(2)}) %collective-permute-start.7) | collective-permute-done | bytes 24608 | tf_op jit(solution)/shard_map/ppermute | solution.py:112
  57.3 0.8 gather_fusion
  58.2 0.8 copy_select_fusion.4
  59.1 1.9 %fusion.29 = f32[2,2,96,1280]{3,2,1,0:T(8,128)S(1)} fusion(bf16[2,2,96,256]{3,2,1,0:T(8,128)(2,1)S(1)} %bitcast.200, f32[256,128]{1,0:T(8,128)} %get-tuple-element.17, f32[256,128]{1,0:T(8,128)} %get-tuple-element.55, f32[256,1024]{1,0:T(8,128)} %get-tuple-element.9, f32[256]{0:T(256)} %copy-done.12), kind=kOutput, calls=%fused_computation.47 | convolution fusion | flops 252968960 | bytes 3474432 | tf_op jit(solution)/shard_map/yxmk,kn->yxmn/dot_general | solution.py:155
  61.5 1.5 %convolution_add_fusion = f32[2,2,96,1280]{3,2,1,0:T(8,128)S(1)} fusion(f32[2,2,96,1280]{3,2,1,0:T(8,128)S(1)} %fusion.29, bf16[2,2,96,256]{3,2,1,0:T(8,128)(2,1)S(1)} %collective-permute-done.8, bf16[256,1280]{1,0:T(8,128)(2,1)} %collective-permute-done.15), kind=kOutput, calls=%fused_computation.12 | convolution fusion | flops 252149760 | bytes 4784128 | tf_op jit(solution)/shard_map/yxmk,kn->yxmn/dot_general | solution.py:155
  63.2 1.5 %convolution_add_fusion.1 = f32[2,2,96,1280]{3,2,1,0:T(8,128)S(1)} fusion(f32[2,2,96,1280]{3,2,1,0:T(8,128)S(1)} %fusion.32, bf16[2,2,96,256]{3,2,1,0:T(8,128)(2,1)S(1)} %collective-permute-done.8, bf16[256,1280]{1,0:T(8,128)(2,1)} %collective-permute-done.9), kind=kOutput, calls=%fused_computation.13 | convolution fusion | flops 252149760 | bytes 4784128 | tf_op jit(solution)/shard_map/yxmk,kn->yxmn/dot_general | solution.py:155
  64.9 11.9 %collective-permute-done.16 = bf16[2,96,1280]{2,1,0:T(8,128)(2,1)S(1)} collective-permute-done((bf16[2,96,1280]{2,1,0:T(8,128)(2,1)S(1)}, bf16[2,96,1280]{2,1,0:T(8,128)(2,1)S(1)}, u32[]{:S(2)}, u32[]{:S(2)}) %collective-permute-start.16) | collective-permute-done | bytes 491552 | tf_op jit(solution)/shard_map/ppermute | solution.py:112
  77.0 1.5 %collective-permute-done.10 = bf16[2,96,1280]{2,1,0:T(8,128)(2,1)S(1)} collective-permute-done((bf16[2,96,1280]{2,1,0:T(8,128)(2,1)S(1)}, bf16[2,96,1280]{2,1,0:T(8,128)(2,1)S(1)}, u32[]{:S(2)}, u32[]{:S(2)}) %collective-permute-start.10) | collective-permute-done | bytes 491552 | tf_op jit(solution)/shard_map/ppermute | solution.py:112
  78.6 2.2 %collective-permute-start.11 = (bf16[96,1280]{1,0:T(8,128)(2,1)S(1)}, bf16[96,1280]{1,0:T(8,128)(2,1)S(1)}, u32[]{:S(2)}, u32[]{:S(2)}) collective-permute-start(bf16[96,1280]{1,0:T(8,128)(2,1)S(1)} %fusion.40), channel_id=1, source_target_pairs={{0,4},{1,5},{2,6},{3,7},{4,0},{5,1},{6,2},{7,3},{8,12},{9,13},{10,... | collective-permute-start | bytes 737288 | tf_op jit(solution)/shard_map/ppermute | solution.py:112
  80.8 3.6 %collective-permute-done.17 = bf16[96,1280]{1,0:T(8,128)(2,1)S(1)} collective-permute-done((bf16[96,1280]{1,0:T(8,128)(2,1)S(1)}, bf16[96,1280]{1,0:T(8,128)(2,1)S(1)}, u32[]{:S(2)}, u32[]{:S(2)}) %collective-permute-start.17) | collective-permute-done | bytes 245792 | tf_op jit(solution)/shard_map/ppermute | solution.py:112
  85.1 3.9 %collective-permute-start.20 = (bf16[24,1280]{1,0:T(8,128)(2,1)S(1)}, bf16[24,1280]{1,0:T(8,128)(2,1)S(1)}, u32[]{:S(2)}, u32[]{:S(2)}) collective-permute-start(bf16[24,1280]{1,0:T(8,128)(2,1)S(1)} %get-tuple-element.19), channel_id=1, source_target_pairs={{0,24},{1,25},{2,26},{3,27},{4,28},{5,29},{6,30},{7,31},{8,16},{9,... | collective-permute-start | bytes 184328 | tf_op jit(solution)/shard_map/ppermute | solution.py:112
  89.0 0.7 fusion.56
  90.3 3.8 %collective-permute-start.14 = (bf16[24,1280]{1,0:T(8,128)(2,1)S(1)}, bf16[24,1280]{1,0:T(8,128)(2,1)}, u32[]{:S(2)}, u32[]{:S(2)}) collective-permute-start(bf16[24,1280]{1,0:T(8,128)(2,1)S(1)} %get-tuple-element.22), channel_id=1, source_target_pairs={{0,24},{1,25},{2,26},{3,27},{4,28},{5,29},{6,30},{7,31},{8,16},{9,... | collective-permute-start | bytes 184328 | tf_op jit(solution)/shard_map/ppermute | solution.py:112
  94.2 1.4 %collective-permute-done.12 = bf16[24,1280]{1,0:T(8,128)(2,1)S(1)} collective-permute-done((bf16[24,1280]{1,0:T(8,128)(2,1)}, bf16[24,1280]{1,0:T(8,128)(2,1)S(1)}, u32[]{:S(2)}, u32[]{:S(2)}) %collective-permute-start.12) | collective-permute-done | bytes 61472 | tf_op jit(solution)/shard_map/ppermute | solution.py:112
  95.6 1.6 %collective-permute-done.14 = bf16[24,1280]{1,0:T(8,128)(2,1)} collective-permute-done((bf16[24,1280]{1,0:T(8,128)(2,1)S(1)}, bf16[24,1280]{1,0:T(8,128)(2,1)}, u32[]{:S(2)}, u32[]{:S(2)}) %collective-permute-start.14) | collective-permute-done | bytes 61472 | tf_op jit(solution)/shard_map/ppermute | solution.py:112
  97.2 0.9 fusion.52
  98.4 1.3 %collective-permute-done.21 = f32[2,12,1280]{2,0,1:T(2,128)S(1)} collective-permute-done((f32[2,12,1280]{2,0,1:T(2,128)S(1)}, f32[2,12,1280]{2,0,1:T(2,128)S(1)}, u32[]{:S(2)}, u32[]{:S(2)}) %collective-permute-start.21) | collective-permute-done | bytes 122912 | tf_op jit(solution)/shard_map/ppermute | solution.py:112
  101.0 0.6 fusion.86
  101.6 3.4 %bitcast_reduce_fusion = (f32[3,4,4,8]{3,1,2,0:T(4,128)S(1)}, f32[3,4,8,128,4,8]{3,5,4,2,1,0:T(8,128)S(1)}) fusion(bf16[3,8,4,128,128]{4,3,2,1,0:T(8,128)(2,1)} %bitcast.198, pred[3,8]{1,0:T(4,128)(4,1)S(1)} %copy-done.25, pred[3,8,128]{2,1,0:T(8,128)(4,1)S(1)} %copy-done.15, bf16[3,4,4,8,128]{4,3,2,1,0:T(8,128)(2,1)S(1)} %fusion.46), kind=kOutput, calls=%fused_computation.15 | convolution fusion | flops 103415424 | bytes 4821528 | tf_op jit(solution)/shard_map/rtkgd,rmknd->rtkgmn/dot_general | solution.py:38
  105.6 1.0 fusion.17
  107.0 0.7 convert_element_type.212
  (154 shorter events, 8.2 us)
Async XLA Ops:
  0.0 20.8 %copy-start = (bf16[16,4,128,128]{3,2,1,0:T(8,128)(2,1)S(1)}, bf16[16,4,128,128]{3,2,1,0:T(8,128)(2,1)}, u32[]{:S(2)}) copy-start(bf16[16,4,128,128]{3,2,1,0:T(8,128)(2,1)} %param.22) | copy-start | bytes 6291460
  0.9 4.6 %copy-start.12 = (f32[256]{0:T(256)}, f32[256]{0:T(256)S(1)}, u32[]{:S(2)}) copy-start(f32[256]{0:T(256)S(1)} %dynamic_slice.146) | copy-start | bytes 3076
  0.9 3.7 %copy-start.3 = (f32[256,512]{1,0:T(8,128)S(1)}, f32[256,512]{1,0:T(8,128)}, u32[]{:S(2)}) copy-start(f32[256,512]{1,0:T(8,128)} %param.18) | copy-start | bytes 1572868
  0.9 3.7 %copy-start.4 = (f32[256,512]{1,0:T(8,128)S(1)}, f32[256,512]{1,0:T(8,128)}, u32[]{:S(2)}) copy-start(f32[256,512]{1,0:T(8,128)} %param.17) | copy-start | bytes 1572868
  5.5 1.9 %copy-start.2 = (bf16[12,4,2048]{2,1,0:T(4,128)(2,1)S(1)}, bf16[12,4,2048]{2,1,0:T(4,128)(2,1)}, u32[]{:S(2)}) copy-start(bf16[12,4,2048]{2,1,0:T(4,128)(2,1)} %param.14) | copy-start | bytes 589828
  5.5 3.6 %copy-start.14 = (f32[1024]{0:T(1024)S(1)}, f32[1024]{0:T(1024)}, u32[]{:S(2)}) copy-start(f32[1024]{0:T(1024)} %param.19) | copy-start | bytes 12292
  5.5 3.6 %copy-start.21 = (f32[128]{0:T(128)S(1)}, f32[128]{0:T(128)}, u32[]{:S(2)}) copy-start(f32[128]{0:T(128)} %param.21) | copy-start | bytes 1540
  5.5 3.6 %copy-start.22 = (f32[128]{0:T(128)S(1)}, f32[128]{0:T(128)}, u32[]{:S(2)}) copy-start(f32[128]{0:T(128)} %param.20) | copy-start | bytes 1540
  5.6 11.7 %copy-start.20 = (s32[3,8]{1,0:T(4,128)S(1)}, s32[3,8]{1,0:T(4,128)}, u32[]{:S(2)}) copy-start(s32[3,8]{1,0:T(4,128)} %param.25) | copy-start | bytes 292
  5.6 12.9 %copy-start.23 = (s32[3]{0:T(128)S(1)}, s32[3]{0:T(128)}, u32[]{:S(2)}) copy-start(s32[3]{0:T(128)} %param.24) | copy-start | bytes 40
  6.9 54.6 %collective-permute-start.15 = (bf16[256,1280]{1,0:T(8,128)(2,1)}, bf16[256,1280]{1,0:T(8,128)(2,1)}, u32[]{:S(2)}, u32[]{:S(2)}) collective-permute-start(bf16[256,1280]{1,0:T(8,128)(2,1)} %get-tuple-element.49), channel_id=1, source_target_pairs={{0,1},{1,0},{2,3},{3,2},{4,5},{5,4},{6,7},{7,6},{8,9},{9,8},{10,11... | collective-permute-start | bytes 1966088 | tf_op jit(solution)/shard_map/ppermute | solution.py:112
  8.1 29.6 %collective-permute-start = (bf16[12,4,256]{2,1,0:T(4,128)(2,1)S(1)}, bf16[12,4,256]{2,1,0:T(4,128)(2,1)S(1)}, u32[]{:S(2)}, u32[]{:S(2)}) collective-permute-start(bf16[12,4,256]{2,1,0:T(4,128)(2,1)S(1)} %get-tuple-element.37), channel_id=1, source_target_pairs={{0,0},{1,8},{2,16},{3,24},{4,1},{5,9},{6,17},{7,25},{8,2},{9,10},{... | collective-permute-start | bytes 73736 | tf_op jit(solution)/shard_map/ppermute | solution.py:112
  9.2 18.7 %collective-permute-start.22 = (f32[1292]{0:T(1024)S(1)}, f32[1292]{0:T(1024)S(1)}, u32[]{:S(2)}, u32[]{:S(2)}) collective-permute-start(f32[1292]{0:T(1024)S(1)} %get-tuple-element.42), channel_id=1, source_target_pairs={{0,1},{1,0},{2,3},{3,2},{4,5},{5,4},{6,7},{7,6},{8,9},{9,8},{10,11... | collective-permute-start | bytes 15512 | tf_op jit(solution)/shard_map/ppermute | solution.py:112
  13.1 14.9 %collective-permute-start.23 = (f32[1292]{0:T(1024)S(1)}, f32[1292]{0:T(1024)S(1)}, u32[]{:S(2)}, u32[]{:S(2)}) collective-permute-start(f32[1292]{0:T(1024)S(1)} %get-tuple-element.43), channel_id=1, source_target_pairs={{0,2},{1,3},{2,0},{3,1},{4,6},{5,7},{6,4},{7,5},{8,10},{9,11},{10,... | collective-permute-start | bytes 15512 | tf_op jit(solution)/shard_map/ppermute | solution.py:112
  16.6 14.0 %collective-permute-start.24 = (f32[1292]{0:T(1024)S(1)}, f32[1292]{0:T(1024)S(1)}, u32[]{:S(2)}, u32[]{:S(2)}) collective-permute-start(f32[1292]{0:T(1024)S(1)} %get-tuple-element.44), channel_id=1, source_target_pairs={{0,3},{1,2},{2,1},{3,0},{4,7},{5,6},{6,5},{7,4},{8,11},{9,10},{10,... | collective-permute-start | bytes 15512 | tf_op jit(solution)/shard_map/ppermute | solution.py:112
  23.6 16.1 %copy-start.10 = (bf16[12,4,256]{2,1,0:T(4,128)(2,1)S(1)}, bf16[12,4,256]{2,1,0:T(4,128)(2,1)}, u32[]{:S(2)}) copy-start(bf16[12,4,256]{2,1,0:T(4,128)(2,1)} %get-tuple-element.32) | copy-start | bytes 73732
  23.6 19.2 %copy-start.9 = (bf16[12,4,256]{2,1,0:T(4,128)(2,1)S(1)}, bf16[12,4,256]{2,1,0:T(4,128)(2,1)}, u32[]{:S(2)}) copy-start(bf16[12,4,256]{2,1,0:T(4,128)(2,1)} %get-tuple-element.31) | copy-start | bytes 73732
  23.6 27.1 %copy-start.8 = (bf16[12,4,256]{2,1,0:T(4,128)(2,1)S(1)}, bf16[12,4,256]{2,1,0:T(4,128)(2,1)}, u32[]{:S(2)}) copy-start(bf16[12,4,256]{2,1,0:T(4,128)(2,1)} %get-tuple-element.30) | copy-start | bytes 73732
  27.9 11.8 %collective-permute-start.1 = (bf16[12,4,256]{2,1,0:T(4,128)(2,1)}, bf16[12,4,256]{2,1,0:T(4,128)(2,1)S(1)}, u32[]{:S(2)}, u32[]{:S(2)}) collective-permute-start(bf16[12,4,256]{2,1,0:T(4,128)(2,1)} %get-tuple-element.36), channel_id=1, source_target_pairs={{0,1},{1,9},{2,17},{3,25},{4,0},{5,8},{6,16},{7,24},{8,3},{9,11},{... | collective-permute-start | bytes 73736 | tf_op jit(solution)/shard_map/ppermute | solution.py:112
  28.0 14.8 %collective-permute-start.2 = (bf16[12,4,256]{2,1,0:T(4,128)(2,1)}, bf16[12,4,256]{2,1,0:T(4,128)(2,1)S(1)}, u32[]{:S(2)}, u32[]{:S(2)}) collective-permute-start(bf16[12,4,256]{2,1,0:T(4,128)(2,1)} %get-tuple-element.35), channel_id=1, source_target_pairs={{0,2},{1,10},{2,18},{3,26},{4,3},{5,11},{6,19},{7,27},{8,0},{9,8},... | collective-permute-start | bytes 73736 | tf_op jit(solution)/shard_map/ppermute | solution.py:112
  30.7 20.0 %collective-permute-start.3 = (bf16[12,4,256]{2,1,0:T(4,128)(2,1)}, bf16[12,4,256]{2,1,0:T(4,128)(2,1)S(1)}, u32[]{:S(2)}, u32[]{:S(2)}) collective-permute-start(bf16[12,4,256]{2,1,0:T(4,128)(2,1)} %get-tuple-element.34), channel_id=1, source_target_pairs={{0,3},{1,11},{2,19},{3,27},{4,2},{5,10},{6,18},{7,26},{8,1},{9,9},... | collective-permute-start | bytes 73736 | tf_op jit(solution)/shard_map/ppermute | solution.py:112
  38.4 12.7 %collective-permute-start.4 = (bf16[12,4,256]{2,1,0:T(4,128)(2,1)}, bf16[12,4,256]{2,1,0:T(4,128)(2,1)S(1)}, u32[]{:S(2)}, u32[]{:S(2)}) collective-permute-start(bf16[12,4,256]{2,1,0:T(4,128)(2,1)} %get-tuple-element.33), channel_id=1, source_target_pairs={{0,4},{1,12},{2,20},{3,28},{4,5},{5,13},{6,21},{7,29},{8,6},{9,14}... | collective-permute-start | bytes 73736 | tf_op jit(solution)/shard_map/ppermute | solution.py:112
  39.7 11.5 %collective-permute-start.5 = (bf16[12,4,256]{2,1,0:T(4,128)(2,1)S(1)}, bf16[12,4,256]{2,1,0:T(4,128)(2,1)S(1)}, u32[]{:S(2)}, u32[]{:S(2)}) collective-permute-start(bf16[12,4,256]{2,1,0:T(4,128)(2,1)S(1)} %copy-done.10), channel_id=1, source_target_pairs={{0,5},{1,13},{2,21},{3,29},{4,4},{5,12},{6,20},{7,28},{8,7},{9,15}... | collective-permute-start | bytes 73736 | tf_op jit(solution)/shard_map/ppermute | solution.py:112
  42.8 10.2 %collective-permute-start.6 = (bf16[12,4,256]{2,1,0:T(4,128)(2,1)S(1)}, bf16[12,4,256]{2,1,0:T(4,128)(2,1)S(1)}, u32[]{:S(2)}, u32[]{:S(2)}) collective-permute-start(bf16[12,4,256]{2,1,0:T(4,128)(2,1)S(1)} %copy-done.9), channel_id=1, source_target_pairs={{0,6},{1,14},{2,22},{3,30},{4,7},{5,15},{6,23},{7,31},{8,4},{9,12}... | collective-permute-start | bytes 73736 | tf_op jit(solution)/shard_map/ppermute | solution.py:112
  50.7 6.6 %collective-permute-start.7 = (bf16[12,4,256]{2,1,0:T(4,128)(2,1)S(1)}, bf16[12,4,256]{2,1,0:T(4,128)(2,1)S(1)}, u32[]{:S(2)}, u32[]{:S(2)}) collective-permute-start(bf16[12,4,256]{2,1,0:T(4,128)(2,1)S(1)} %copy-done.8), channel_id=1, source_target_pairs={{0,7},{1,15},{2,23},{3,31},{4,6},{5,14},{6,22},{7,30},{8,5},{9,13}... | collective-permute-start | bytes 73736 | tf_op jit(solution)/shard_map/ppermute | solution.py:112
  51.1 12.1 %collective-permute-start.9 = (bf16[256,1280]{1,0:T(8,128)(2,1)}, bf16[256,1280]{1,0:T(8,128)(2,1)}, u32[]{:S(2)}, u32[]{:S(2)}) collective-permute-start(bf16[256,1280]{1,0:T(8,128)(2,1)} %get-tuple-element.50), channel_id=1, source_target_pairs={{0,1},{1,0},{2,3},{3,2},{4,5},{5,4},{6,7},{7,6},{8,9},{9,8},{10,11... | collective-permute-start | bytes 1966088 | tf_op jit(solution)/shard_map/ppermute | solution.py:112
  58.9 2.6 %collective-permute-start.8 = (bf16[2,2,96,256]{3,2,1,0:T(8,128)(2,1)S(1)}, bf16[2,2,96,256]{3,2,1,0:T(8,128)(2,1)S(1)}, u32[]{:S(2)}, u32[]{:S(2)}) collective-permute-start(bf16[2,2,96,256]{3,2,1,0:T(8,128)(2,1)S(1)} %bitcast.199), channel_id=1, source_target_pairs={{0,1},{1,0},{2,3},{3,2},{4,5},{5,4},{6,7},{7,6},{8,9},{9,8},{10,11... | collective-permute-start | bytes 589832 | tf_op jit(solution)/shard_map/ppermute | solution.py:112
  59.0 1.9 %copy-start.5 = (f32[256,128]{1,0:T(8,128)S(1)}, f32[256,128]{1,0:T(8,128)}, u32[]{:S(2)}) copy-start(f32[256,128]{1,0:T(8,128)} %get-tuple-element.16) | copy-start | bytes 393220
  59.0 1.9 %copy-start.6 = (f32[256,128]{1,0:T(8,128)S(1)}, f32[256,128]{1,0:T(8,128)}, u32[]{:S(2)}) copy-start(f32[256,128]{1,0:T(8,128)} %get-tuple-element.56) | copy-start | bytes 393220
  59.0 1.9 %copy-start.13 = (f32[256]{0:T(256)S(1)}, f32[256]{0:T(256)}, u32[]{:S(2)}) copy-start(f32[256]{0:T(256)} %copy-done.12) | copy-start | bytes 3076
  63.1 13.7 %collective-permute-start.16 = (bf16[2,96,1280]{2,1,0:T(8,128)(2,1)S(1)}, bf16[2,96,1280]{2,1,0:T(8,128)(2,1)S(1)}, u32[]{:S(2)}, u32[]{:S(2)}) collective-permute-start(bf16[2,96,1280]{2,1,0:T(8,128)(2,1)S(1)} %fusion.39), channel_id=1, source_target_pairs={{0,4},{1,5},{2,6},{3,7},{4,0},{5,1},{6,2},{7,3},{8,12},{9,13},{10,... | collective-permute-start | bytes 1474568 | tf_op jit(solution)/shard_map/ppermute | solution.py:112
  64.8 13.7 %collective-permute-start.10 = (bf16[2,96,1280]{2,1,0:T(8,128)(2,1)S(1)}, bf16[2,96,1280]{2,1,0:T(8,128)(2,1)S(1)}, u32[]{:S(2)}, u32[]{:S(2)}) collective-permute-start(bf16[2,96,1280]{2,1,0:T(8,128)(2,1)S(1)} %fusion.38), channel_id=1, source_target_pairs={{0,2},{1,3},{2,0},{3,1},{4,6},{5,7},{6,4},{7,5},{8,10},{9,11},{10,... | collective-permute-start | bytes 1474568 | tf_op jit(solution)/shard_map/ppermute | solution.py:112
  76.9 7.5 %collective-permute-start.17 = (bf16[96,1280]{1,0:T(8,128)(2,1)S(1)}, bf16[96,1280]{1,0:T(8,128)(2,1)S(1)}, u32[]{:S(2)}, u32[]{:S(2)}) collective-permute-start(bf16[96,1280]{1,0:T(8,128)(2,1)S(1)} %fusion.41), channel_id=1, source_target_pairs={{0,2},{1,3},{2,0},{3,1},{4,6},{5,7},{6,4},{7,5},{8,10},{9,11},{10,... | collective-permute-start | bytes 737288 | tf_op jit(solution)/shard_map/ppermute | solution.py:112
  78.6 10.4 %collective-permute-start.11 = (bf16[96,1280]{1,0:T(8,128)(2,1)S(1)}, bf16[96,1280]{1,0:T(8,128)(2,1)S(1)}, u32[]{:S(2)}, u32[]{:S(2)}) collective-permute-start(bf16[96,1280]{1,0:T(8,128)(2,1)S(1)} %fusion.40), channel_id=1, source_target_pairs={{0,4},{1,5},{2,6},{3,7},{4,0},{5,1},{6,2},{7,3},{8,12},{9,13},{10,... | collective-permute-start | bytes 737288 | tf_op jit(solution)/shard_map/ppermute | solution.py:112
  84.5 5.8 %collective-permute-start.18 = (bf16[24,1280]{1,0:T(8,128)(2,1)S(1)}, bf16[24,1280]{1,0:T(8,128)(2,1)S(1)}, u32[]{:S(2)}, u32[]{:S(2)}) collective-permute-start(bf16[24,1280]{1,0:T(8,128)(2,1)S(1)} %get-tuple-element.18), channel_id=1, source_target_pairs={{0,8},{1,9},{2,10},{3,11},{4,12},{5,13},{6,14},{7,15},{8,0},{9,1},... | collective-permute-start | bytes 184328 | tf_op jit(solution)/shard_map/ppermute | solution.py:112
  84.6 9.6 %collective-permute-start.19 = (bf16[24,1280]{1,0:T(8,128)(2,1)S(1)}, bf16[24,1280]{1,0:T(8,128)(2,1)S(1)}, u32[]{:S(2)}, u32[]{:S(2)}) collective-permute-start(bf16[24,1280]{1,0:T(8,128)(2,1)S(1)} %get-tuple-element.20), channel_id=1, source_target_pairs={{0,16},{1,17},{2,18},{3,19},{4,20},{5,21},{6,22},{7,23},{8,24},{9,... | collective-permute-start | bytes 184328 | tf_op jit(solution)/shard_map/ppermute | solution.py:112
  85.1 9.1 %collective-permute-start.20 = (bf16[24,1280]{1,0:T(8,128)(2,1)S(1)}, bf16[24,1280]{1,0:T(8,128)(2,1)S(1)}, u32[]{:S(2)}, u32[]{:S(2)}) collective-permute-start(bf16[24,1280]{1,0:T(8,128)(2,1)S(1)} %get-tuple-element.19), channel_id=1, source_target_pairs={{0,24},{1,25},{2,26},{3,27},{4,28},{5,29},{6,30},{7,31},{8,16},{9,... | collective-permute-start | bytes 184328 | tf_op jit(solution)/shard_map/ppermute | solution.py:112
  89.7 8.7 %copy-start.16 = (f32[3,4]{1,0:T(4,128)S(1)}, f32[3,4]{1,0:T(4,128)}, u32[]{:S(2)}) copy-start(f32[3,4]{1,0:T(4,128)} %squeeze.60) | copy-start | bytes 148
  89.7 8.7 %copy-start.17 = (f32[3,4]{1,0:T(4,128)S(1)}, f32[3,4]{1,0:T(4,128)}, u32[]{:S(2)}) copy-start(f32[3,4]{1,0:T(4,128)} %slice.64) | copy-start | bytes 148
  89.7 8.7 %copy-start.18 = (f32[3,4]{1,0:T(4,128)S(1)}, f32[3,4]{1,0:T(4,128)}, u32[]{:S(2)}) copy-start(f32[3,4]{1,0:T(4,128)} %slice.66) | copy-start | bytes 148
  89.7 8.7 %copy-start.19 = (f32[3,4]{1,0:T(4,128)S(1)}, f32[3,4]{1,0:T(4,128)}, u32[]{:S(2)}) copy-start(f32[3,4]{1,0:T(4,128)} %slice.68) | copy-start | bytes 148
  89.7 5.9 %collective-permute-start.12 = (bf16[24,1280]{1,0:T(8,128)(2,1)}, bf16[24,1280]{1,0:T(8,128)(2,1)S(1)}, u32[]{:S(2)}, u32[]{:S(2)}) collective-permute-start(bf16[24,1280]{1,0:T(8,128)(2,1)} %get-tuple-element.21), channel_id=1, source_target_pairs={{0,8},{1,9},{2,10},{3,11},{4,12},{5,13},{6,14},{7,15},{8,0},{9,1},... | collective-permute-start | bytes 184328 | tf_op jit(solution)/shard_map/ppermute | solution.py:112
  89.8 5.8 %collective-permute-start.13 = (bf16[24,1280]{1,0:T(8,128)(2,1)S(1)}, bf16[24,1280]{1,0:T(8,128)(2,1)S(1)}, u32[]{:S(2)}, u32[]{:S(2)}) collective-permute-start(bf16[24,1280]{1,0:T(8,128)(2,1)S(1)} %get-tuple-element.23), channel_id=1, source_target_pairs={{0,16},{1,17},{2,18},{3,19},{4,20},{5,21},{6,22},{7,23},{8,24},{9,... | collective-permute-start | bytes 184328 | tf_op jit(solution)/shard_map/ppermute | solution.py:112
  90.3 6.9 %collective-permute-start.14 = (bf16[24,1280]{1,0:T(8,128)(2,1)S(1)}, bf16[24,1280]{1,0:T(8,128)(2,1)}, u32[]{:S(2)}, u32[]{:S(2)}) collective-permute-start(bf16[24,1280]{1,0:T(8,128)(2,1)S(1)} %get-tuple-element.22), channel_id=1, source_target_pairs={{0,24},{1,25},{2,26},{3,27},{4,28},{5,29},{6,30},{7,31},{8,16},{9,... | collective-permute-start | bytes 184328 | tf_op jit(solution)/shard_map/ppermute | solution.py:112
  98.1 2.2 %copy-start.7 = (f32[4,1280]{1,0:T(4,128)S(1)}, f32[4,1280]{1,0:T(4,128)}, u32[]{:S(2)}) copy-start(f32[4,1280]{1,0:T(4,128)} %broadcast_select_fusion) | copy-start | bytes 61444
  98.3 1.4 %collective-permute-start.21 = (f32[2,12,1280]{2,0,1:T(2,128)S(1)}, f32[2,12,1280]{2,0,1:T(2,128)S(1)}, u32[]{:S(2)}, u32[]{:S(2)}) collective-permute-start(f32[2,12,1280]{2,0,1:T(2,128)S(1)} %bitcast.207), channel_id=1, source_target_pairs={{0,1},{1,0},{2,3},{3,2},{4,5},{5,4},{6,7},{7,6},{8,9},{9,8},{10,11... | collective-permute-start | bytes 368648 | tf_op jit(solution)/shard_map/ppermute | solution.py:112
  100.5 1.1 %copy-start.15 = (pred[3,8,128]{2,1,0:T(8,128)(4,1)S(1)}, pred[3,8,128]{2,1,0:T(8,128)(4,1)}, u32[]{:S(2)}) copy-start(pred[3,8,128]{2,1,0:T(8,128)(4,1)} %broadcast_compare_fusion) | copy-start | bytes 9220
  101.6 4.0 %copy-start.1 = (bf16[24,4,128,128]{3,2,1,0:T(8,128)(2,1)S(1)}, bf16[24,4,128,128]{3,2,1,0:T(8,128)(2,1)}, u32[]{:S(2)}) copy-start(bf16[24,4,128,128]{3,2,1,0:T(8,128)(2,1)} %gather_fusion.2) | copy-start | bytes 9437188
  (3 other events, 2.4 us)

commit v2 on v1

--- a/solution.py
+++ b/solution.py
@@ -113,15 +113,18 @@
 
     pick = lambda a, i, axis=0: lax.dynamic_index_in_dim(a, i, axis, keepdims=False)
 
-    got = []
-    for k in range(R):
-        part = lax.dynamic_slice_in_dim(hidden, (ri ^ k) * kw, kw, 2)
-        pairs = [(r * T + t, t * R + (r ^ k)) for r in range(R) for t in range(T)]
-        got.append(send(part, pairs))
-    j = me % R
-    acts = jnp.take(jnp.stack(got), j ^ jnp.arange(R), axis=0)
-    acts = acts.reshape(Z, 2, 2, 2 * own, kw).transpose(1, 2, 0, 3, 4).reshape(2, 2, Z * 2 * own, kw)
-    acts_sib = send(acts, to_core)
+    def both(i, mine, other):
+        return jnp.stack([jnp.where(i == 0, mine, other), jnp.where(i == 0, other, mine)])
+
+    zh, zl = z // 2, z % 2
+    acts = hidden.reshape(T * own, 2, 2, 2, kw).transpose(1, 2, 3, 0, 4)
+    acts = send(acts, perm(lambda z, y, x, c: (z // 2 * 2 + c, y, x, z % 2)))
+    acts = both(x, pick(acts, x, 1), send(pick(acts, 1 - x, 1), to_x))
+    acts = both(y, pick(acts, y, 1), send(pick(acts, 1 - y, 1), to_y))
+    to_far = perm(lambda z, y, x, c: (z ^ 2, y, x, c))
+    acts = both(zh, pick(acts, zh, 1), send(pick(acts, 1 - zh, 1), to_far))
+    acts = both(c, acts, send(acts, to_core))
+    acts_own, acts_sib = pick(acts, c, 3), pick(acts, 1 - c, 3)
 
     gain = lax.dynamic_slice_in_dim(norm_gain, me * kw, kw)[:, None]
 
@@ -138,42 +141,38 @@
     w_sib = [send(columns(1 - c, g), to_core) for g in range(G)]
 
     wide = hidden.astype(F32)
-    power = jnp.sum(wide * wide, axis=2).reshape(T, own)
+    power = jnp.sum(wide * wide, axis=2).reshape(T * own)
     bias = jnp.concatenate([bias_query, bias_key, bias_value])
-    biases = [bias]
-    squares = pick(power, ti)
-    for k in range(1, T):
-        msg = jnp.concatenate([bias, pick(power, ti ^ k)])
-        pairs = [(r * T + t, r * T + (t ^ k)) for r in range(R) for t in range(T)]
-        msg = send(msg, pairs)
-        biases.append(msg[: bias.shape[0]])
-        squares = squares + msg[bias.shape[0] :]
-    bias_all = jnp.take(jnp.stack(biases), ti ^ jnp.arange(T), axis=0)
-    row_scale = lax.rsqrt(squares / D + EPS)
+    there = send(jnp.concatenate([bias, power]), to_x)
+    biases = both(x, bias, there[:gw])
+    power = power + there[gw:]
 
     def dot(g):
-        f = lambda a, w: jnp.einsum("yxmk,kn->yxmn", a, w, preferred_element_type=F32)
-        return f(acts, w_own[g]) + f(acts_sib, w_sib[g])
+        f = lambda a, w: jnp.einsum("abymk,kn->abymn", a, w, preferred_element_type=F32)
+        out = f(acts_own, w_own[g]) + f(acts_sib, w_sib[g])
+        return out.reshape(2, 2, 2, 2, 2 * own, gw)
 
     done = []
     for g in range(G):
         part = dot(g)
-        first, second = ((x, 1, to_x), (y, 0, to_y)) if g % 2 == 0 else ((y, 0, to_y), (x, 0, to_x))
-        i, axis, pairs = first
-        part = pick(part, i, axis) + send(pick(part, 1 - i, axis).astype(BF), pairs).astype(F32)
-        i, axis, pairs = second
-        part = pick(part, i, axis) + send(pick(part, 1 - i, axis).astype(BF), pairs).astype(F32)
-        part = part.reshape(Z, 2 * own, gw)
-        total = pick(part, z)
+        for i, axis, pairs in ((x, 3, to_x), (y, 2, to_y))[:: 1 if g % 2 == 0 else -1]:
+            there = send(pick(part, 1 - i, axis).astype(BF), pairs)
+            part = jnp.expand_dims(pick(part, i, axis) + there.astype(F32), axis)
+        part = part.reshape(2, 2, 2 * own, gw)
+        at = lambda z: pick(pick(part, z % 2), z // 2)
+        total = at(z)
         for k in range(1, Z):
             pairs = perm(lambda z, y, x, c: (z ^ k, y, x, c))
-            total = total + send(pick(part, z ^ k).astype(BF), pairs).astype(F32)
+            total = total + send(at(z ^ k).astype(BF), pairs).astype(F32)
         done.append(total.reshape(2, own, gw))
     done = jnp.stack(done)
-    mine = pick(done, c, 1)
-    other = send(pick(done, 1 - c, 1), to_core)
-    low, high = jnp.where(c == 0, mine, other), jnp.where(c == 0, other, mine)
-    full = jnp.stack([low, high], 1).reshape(KVH, own, gw)
+    mine, other = pick(done, c, 1), pick(done, 1 - c, 1)
+    low = jnp.pad(power, (0, G * gw - T * own)).reshape(G, 1, gw)
+    other = send(jnp.concatenate([other, biases[:, None], low], 1), to_core)
+    full = both(c, mine, other[:, :own]).transpose(1, 0, 2, 3).reshape(KVH, own, gw)
+    bias_all = both(c, biases, other[:, own]).transpose(1, 0, 2).reshape(KVH, gw)
+    power = power + other[:, own + 1].reshape(-1)[: T * own]
+    row_scale = lax.rsqrt(pick(power.reshape(T, own), ti) / D + EPS)
     full = full * row_scale[None, :, None] + bias_all[:, None, :]
     full = full.astype(BF).reshape(KVH, rows, steps, gw)
     query = full[..., :qw].reshape(KVH, rows, steps, HQ // KVH, HD).transpose(1, 2, 0, 3, 4)
@@ -189,7 +188,7 @@
     def on_device(hidden, norm_gain, *rest):
         m = hidden.shape[0] * hidden.shape[1] * R
         few_rows = m * T < norm_gain.shape[0]
-        two_ways = T == KVH and R & (R - 1) == 0 and R > T
+        two_ways = T == KVH and R == 2 * T
         if few_rows and two_ways:
             return sums_plan(R, T, hidden, norm_gain, *rest)
         return weights_plan(hidden, norm_gain, *rest)

time: 108 us -> 93.6 us (0.87)
  starting transfers between devices: 38.5 us -> 23.3 us
  waiting for transfers between devices: 27.3 us -> 33.1 us
  local copies, waits for them, and re-layouts: 21.4 us -> 17.3 us
  matrix products: 10.7 us -> 9.33 us
    ppermute x25 -> x19, starting transfers between devices: 38.5 us -> 23.3 us  [send(): return lax.ppermute(a, AXES, pairs)]
    ppermute x25 -> x19, waiting for transfers between devices: 27.3 us -> 33.1 us  [send(): return lax.ppermute(a, AXES, pairs)]
    another operation x3 -> x7, other arithmetic: 0.28 us -> 2.49 us  [both(): jnp.stack([jnp.where(i == 0, mine, other), jnp.where(i == 0, other, mine)])]
    slice x6 -> x4, local copies, waits for them, and re-layouts: 2.04 us -> 0.17 us  [the longest x3 0.09 us: sums_plan(): power = power + other[:, own + 1].reshape(-1)[:T * own]]
    unnamed x60 -> x37, local copies, waits for them, and re-layouts: 1.57 us -> 0.09 us
    gather x3 -> x0, local copies, waits for them, and re-layouts: 1.46 us -> none  [the longest x2 0.89 us: sums_plan(): acts = jnp.take(jnp.stack(got), j ^ jnp.arange(R), axis=0)]
    select_n x4 -> x2, other arithmetic: 1.44 us -> 0.02 us  [both(): jnp.where(i == 0, mine, other)]
    dot_general x4, matrix products: 5.44 us -> 4.08 us  [dot(): jnp.einsum('abymk,kn->abymn', a, w, preferred_element_type=F32)]
  transfers between devices with their start and end apart: 25 -> 19, of which waited for: 8 -> 10; matrix products, arithmetic and copies ran while one was open for 23% -> 27% of each run, Pallas kernels for 0% -> 0%
where the time goes in v2:
time: 93.6 us; the launch traced here: 93.2 us
  waiting for transfers between devices  33.1 us (35%)
  starting transfers between devices  23.3 us (25%)
  local copies, waits for them, and re-layouts  17.3 us (18%)
  matrix products  9.33 us (10%)
  other arithmetic  9.28 us (10%)
    ppermute x19, waiting for transfers between devices, send(): return lax.ppermute(a, AXES, pairs)  33.1 us
    ppermute x19, starting transfers between devices, send(): return lax.ppermute(a, AXES, pairs)  23.3 us
    gather x1, local copies, waits for them, and re-layouts, attend(): vals = jnp.take(value_pages, page_table, axis=0)  4.27 us
    dot_general x4, matrix products, dot(): jnp.einsum('abymk,kn->abymn', a, w, preferred_element_type=F32)  4.08 us
    dynamic_slice x1, local copies, waits for them, and re-layouts, columns(): lax.dynamic_slice_in_dim(w_query, h * qw, qw, 1)  3.68 us
    dot_general x1, matrix products, attend(): jnp.einsum('rtkgd,rmknd->rtkgmn', q_heads, keys, preferred_element_type=j...  3.35 us
    gather x1, local copies, waits for them, and re-layouts, attend(): keys = jnp.take(key_pages, page_table, axis=0)  2.74 us
    another operation x7, other arithmetic, both(): jnp.stack([jnp.where(i == 0, mine, other), jnp.where(i == 0, other, mine)])  2.49 us
  transfers between devices with their start and end apart: 19, of which 10 were waited for; matrix products, arithmetic and copies ran while one was open for 27% of the time, Pallas kernels for 0%

profile of v2, /device:TPU:0, one launch (start us, length us, event | category | flops | bytes accessed | tf_op | source)
XLA Modules:
  0.0 93.2 jit_solution(13610844892410072352)
XLA Ops:
  0.0 1.2 %reshape.298 = bf16[48,2,2,2,256]{4,3,2,1,0:T(2,128)(2,1)S(1)} reshape(bf16[12,4,2048]{2,1,0:T(4,128)(2,1)} %param.14) | data formatting | bytes 393216 | tf_op jit(solution)/shard_map/reshape | solution.py:120
  1.2 1.3 %collective-permute-start = (bf16[2,2,2,48,256]{4,2,1,0,3:T(2,128)(2,1)S(1)}, bf16[2,2,2,48,256]{4,2,1,0,3:T(2,128)(2,1)}, u32[]{:S(2)}, u32[]{:S(2)}) collective-permute-start(bf16[2,2,2,48,256]{4,2,1,0,3:T(2,128)(2,1)S(1)} %bitcast.237), channel_id=1, source_target_pairs={{0,0},{1,8},{2,2},{3,10},{4,4},{5,12},{6,6},{7,14},{8,1},{9,9},{10... | collective-permute-start | bytes 589832 | tf_op jit(solution)/shard_map/ppermute | solution.py:112
  2.5 0.8 dynamic_slice.140
  3.3 3.7 %constant_dynamic-slice_fusion.5 = (f32[256,1024]{1,0:T(8,128)S(1)}, f32[256,1024]{1,0:T(8,128)S(1)}, f32[256,1024]{1,0:T(8,128)S(1)}, f32[256,1024]{1,0:T(8,128)}) fusion(f32[256,4096]{1,0:T(8,128)} %param.16, s32[]{:T(128)S(6)} %select_n.356, s32[]{:T(128)S(6)} %select_n.330, s32[]{:T(128)S(6)} %select_n.326, s32[]{:T(128)S(6)} %select_n.354), kind=kLoop, calls=%fused_computation.155 | loop fusion | bytes 8388624 | tf_op jit(solution)/shard_map/dynamic_slice | solution.py:134
  7.0 0.9 constant_dynamic-slice_fusion.3
  7.9 1.3 %fusion.15 = (bf16[256,1280]{1,0:T(8,128)(2,1)}, bf16[256,1280]{1,0:T(8,128)(2,1)}) fusion(f32[256,128]{1,0:T(8,128)S(1)} %get-tuple-element.14, f32[256,128]{1,0:T(8,128)S(1)} %get-tuple-element.59, f32[256,1024]{1,0:T(8,128)S(1)} %get-tuple-element.6, f32[256]{0:T(256)S(1)} %dynamic_slice.140, f32[256,128]{1,0:T(8,128)S(1)} %get-tuple-element.15, ...), kind=kLoop, calls=%fused_computation.27 | loop fusion | flops 2621440 | bytes 3933184 | tf_op jit(solution)/shard_map/convert_element_type | solution.py:138
  9.2 3.8 %collective-permute-start.11 = (bf16[256,1280]{1,0:T(8,128)(2,1)}, bf16[256,1280]{1,0:T(8,128)(2,1)}, u32[]{:S(2)}, u32[]{:S(2)}) collective-permute-start(bf16[256,1280]{1,0:T(8,128)(2,1)} %get-tuple-element.50), channel_id=1, source_target_pairs={{0,1},{1,0},{2,3},{3,2},{4,5},{5,4},{6,7},{7,6},{8,9},{9,8},{10,11... | collective-permute-start | bytes 1966088 | tf_op jit(solution)/shard_map/ppermute | solution.py:112
  13.3 1.6 %collective-permute-start.17 = (f32[1328]{0:T(1024)S(1)}, f32[1328]{0:T(1024)S(1)}, u32[]{:S(2)}, u32[]{:S(2)}) collective-permute-start(f32[1328]{0:T(1024)S(1)} %pad_maximum_fusion.3), channel_id=1, source_target_pairs={{0,2},{1,3},{2,0},{3,1},{4,6},{5,7},{6,4},{7,5},{8,10},{9,11},{10,... | collective-permute-start | bytes 15944 | tf_op jit(solution)/shard_map/ppermute | solution.py:112
  15.1 0.7 broadcast_compare_fusion
  16.0 0.5 compare_and_fusion
  16.5 1.0 %dynamic-slice_bitcast_fusion = bf16[2,2,48,256]{3,1,0,2:T(2,128)(2,1)S(1)} fusion(bf16[2,2,2,48,256]{4,2,1,0,3:T(2,128)(2,1)} %collective-permute-done, s32[]{:T(128)S(6)} %select_n.312), kind=kLoop, calls=%fused_computation.128 | loop fusion | bytes 196612 | tf_op jit(solution)/shard_map/jit(dynamic_index_in_dim)/squeeze | solution.py:114
  17.5 0.6 collective-permute-start.1
  18.1 4.4 %collective-permute-done.1 = bf16[2,2,48,256]{3,1,0,2:T(2,128)(2,1)S(1)} collective-permute-done((bf16[2,2,48,256]{3,1,0,2:T(2,128)(2,1)S(1)}, bf16[2,2,48,256]{3,1,0,2:T(2,128)(2,1)S(1)}, u32[]{:S(2)}, u32[]{:S(2)}) %collective-permute-start.1) | collective-permute-done | bytes 98336 | tf_op jit(solution)/shard_map/ppermute | solution.py:112
  22.5 1.1 %fusion.58 = (bf16[1,2,2,48,256]{4,2,1,3,0:T(2,128)(2,1)S(1)}, bf16[1,2,2,48,256]{4,2,1,3,0:T(2,128)(2,1)S(1)}) fusion(bf16[2,2,48,256]{3,1,0,2:T(2,128)(2,1)S(1)} %collective-permute-done.1, pred[]{:T(512)S(6)} %eq.36, bf16[2,2,2,48,256]{4,2,1,0,3:T(2,128)(2,1)} %collective-permute-done, s32[]{:T(128)S(6)} %select_n.311), kind=kLoop, calls=%fused_computation.112 | loop fusion | flops 98304 | bytes 393221 | tf_op jit(solution)/shard_map/stack | solution.py:117
  23.8 1.6 %collective-permute-start.2 = (bf16[2,2,48,256]{3,2,1,0:T(8,128)(2,1)S(1)}, bf16[2,2,48,256]{3,2,1,0:T(8,128)(2,1)S(1)}, u32[]{:S(2)}, u32[]{:S(2)}) collective-permute-start(bf16[2,2,48,256]{3,2,1,0:T(8,128)(2,1)S(1)} %bitcast.238), channel_id=1, source_target_pairs={{0,4},{1,5},{2,6},{3,7},{4,0},{5,1},{6,2},{7,3},{8,12},{9,13},{10,... | collective-permute-start | bytes 294920 | tf_op jit(solution)/shard_map/ppermute | solution.py:112
  25.4 3.1 %collective-permute-done.2 = bf16[2,2,48,256]{3,2,1,0:T(8,128)(2,1)S(1)} collective-permute-done((bf16[2,2,48,256]{3,2,1,0:T(8,128)(2,1)S(1)}, bf16[2,2,48,256]{3,2,1,0:T(8,128)(2,1)S(1)}, u32[]{:S(2)}, u32[]{:S(2)}) %collective-permute-start.2) | collective-permute-done | bytes 98336 | tf_op jit(solution)/shard_map/ppermute | solution.py:112
  28.6 0.7 fusion.60
  29.2 2.6 %collective-permute-start.3 = (bf16[2,2,48,256]{3,2,0,1:T(8,128)(2,1)}, bf16[2,2,48,256]{3,2,0,1:T(8,128)(2,1)}, u32[]{:S(2)}, u32[]{:S(2)}) collective-permute-start(bf16[2,2,48,256]{3,2,0,1:T(8,128)(2,1)} %fusion.60), channel_id=1, source_target_pairs={{0,16},{1,17},{2,18},{3,19},{4,20},{5,21},{6,22},{7,23},{8,24},{9,... | collective-permute-start | bytes 294920 | tf_op jit(solution)/shard_map/ppermute | solution.py:112
  31.8 0.5 fusion.98
  32.4 3.2 %collective-permute-done.3 = bf16[2,2,48,256]{3,2,0,1:T(8,128)(2,1)} collective-permute-done((bf16[2,2,48,256]{3,2,0,1:T(8,128)(2,1)}, bf16[2,2,48,256]{3,2,0,1:T(8,128)(2,1)}, u32[]{:S(2)}, u32[]{:S(2)}) %collective-permute-start.3) | collective-permute-done | bytes 98336 | tf_op jit(solution)/shard_map/ppermute | solution.py:112
  35.6 0.9 select_bitcast_fusion.3
  36.7 1.4 %collective-permute-done.4 = bf16[2,2,2,48,256]{4,3,1,0,2:T(8,128)(2,1)S(1)} collective-permute-done((bf16[2,2,2,48,256]{4,3,1,0,2:T(8,128)(2,1)S(1)}, bf16[2,2,2,48,256]{4,3,1,0,2:T(8,128)(2,1)S(1)}, u32[]{:S(2)}, u32[]{:S(2)}) %collective-permute-start.4) | collective-permute-done | bytes 196640 | tf_op jit(solution)/shard_map/ppermute | solution.py:112
  38.1 0.5 fusion.29
  38.7 1.6 %convolution_add_fusion = f32[2,2,2,48,1280]{4,3,2,1,0:T(8,128)S(1)} fusion(f32[2,2,2,48,1280]{4,3,2,1,0:T(8,128)S(1)} %fusion.29, bf16[256,1280]{1,0:T(8,128)(2,1)} %collective-permute-done.11, s32[]{:T(128)S(6)} %select_n.329, bf16[1,2,2,2,48,256]{5,4,2,1,0,3:T(8,128)(2,1)S(1)} %get-tuple-element.25, bf16[1,2,2,2,48,256]{5,4,2,1,0,3:T(8,128)(2,1)S(1)} %get-tuple-element.24), kind=kOutput, calls=%fused_computation.10 | convolution fusion | flops 252248064 | bytes 4980740 | tf_op jit(solution)/shard_map/abymk,kn->abymn/dot_general | solution.py:151
  40.3 1.6 %collective-permute-start.12 = (bf16[2,2,2,24,1280]{4,3,2,1,0:T(8,128)(2,1)S(1)}, bf16[2,2,2,24,1280]{4,3,2,1,0:T(8,128)(2,1)S(1)}, u32[]{:S(2)}, u32[]{:S(2)}) collective-permute-start(bf16[2,2,2,24,1280]{4,3,2,1,0:T(8,128)(2,1)S(1)} %fusion.39), channel_id=1, source_target_pairs={{0,4},{1,5},{2,6},{3,7},{4,0},{5,1},{6,2},{7,3},{8,12},{9,13},{10,... | collective-permute-start | bytes 1474568 | tf_op jit(solution)/shard_map/ppermute | solution.py:112
  41.9 0.5 fusion.32
  42.4 1.5 %convolution_add_fusion.1 = f32[2,2,2,48,1280]{4,3,2,1,0:T(8,128)S(1)} fusion(f32[2,2,2,48,1280]{4,3,2,1,0:T(8,128)S(1)} %fusion.32, bf16[256,1280]{1,0:T(8,128)(2,1)} %collective-permute-done.5, s32[]{:T(128)S(6)} %select_n.329, bf16[1,2,2,2,48,256]{5,4,2,1,0,3:T(8,128)(2,1)S(1)} %get-tuple-element.25, ...), kind=kOutput, calls=%fused_computation.11 | convolution fusion | flops 252248064 | bytes 4980740 | tf_op jit(solution)/shard_map/abymk,kn->abymn/dot_general | solution.py:151
  44.0 0.6 collective-permute-start.6
  44.6 9.0 %collective-permute-done.12 = bf16[2,2,2,24,1280]{4,3,2,1,0:T(8,128)(2,1)S(1)} collective-permute-done((bf16[2,2,2,24,1280]{4,3,2,1,0:T(8,128)(2,1)S(1)}, bf16[2,2,2,24,1280]{4,3,2,1,0:T(8,128)(2,1)S(1)}, u32[]{:S(2)}, u32[]{:S(2)}) %collective-permute-start.12) | collective-permute-done | bytes 491552 | tf_op jit(solution)/shard_map/ppermute | solution.py:112
  53.8 0.6 collective-permute-start.13
  54.4 3.8 %collective-permute-done.6 = bf16[2,2,2,24,1280]{4,3,2,1,0:T(8,128)(2,1)S(1)} collective-permute-done((bf16[2,2,2,24,1280]{4,3,2,1,0:T(8,128)(2,1)S(1)}, bf16[2,2,2,24,1280]{4,3,2,1,0:T(8,128)(2,1)S(1)}, u32[]{:S(2)}, u32[]{:S(2)}) %collective-permute-start.6) | collective-permute-done | bytes 491552 | tf_op jit(solution)/shard_map/ppermute | solution.py:112
  58.4 3.9 %collective-permute-done.13 = bf16[2,2,1,24,1280]{4,3,2,1,0:T(8,128)(2,1)S(1)} collective-permute-done((bf16[2,2,1,24,1280]{4,3,2,1,0:T(8,128)(2,1)S(1)}, bf16[2,2,1,24,1280]{4,3,2,1,0:T(8,128)(2,1)S(1)}, u32[]{:S(2)}, u32[]{:S(2)}) %collective-permute-start.13) | collective-permute-done | bytes 245792 | tf_op jit(solution)/shard_map/ppermute | solution.py:112
  62.5 2.1 %collective-permute-start.15 = (bf16[24,1280]{1,0:T(8,128)(2,1)S(1)}, bf16[24,1280]{1,0:T(8,128)(2,1)S(1)}, u32[]{:S(2)}, u32[]{:S(2)}) collective-permute-start(bf16[24,1280]{1,0:T(8,128)(2,1)S(1)} %get-tuple-element.20), channel_id=1, source_target_pairs={{0,16},{1,17},{2,18},{3,19},{4,20},{5,21},{6,22},{7,23},{8,24},{9,... | collective-permute-start | bytes 184328 | tf_op jit(solution)/shard_map/ppermute | solution.py:112
  64.6 2.3 %collective-permute-start.16 = (bf16[24,1280]{1,0:T(8,128)(2,1)S(1)}, bf16[24,1280]{1,0:T(8,128)(2,1)S(1)}, u32[]{:S(2)}, u32[]{:S(2)}) collective-permute-start(bf16[24,1280]{1,0:T(8,128)(2,1)S(1)} %get-tuple-element.19), channel_id=1, source_target_pairs={{0,24},{1,25},{2,26},{3,27},{4,28},{5,29},{6,30},{7,31},{8,16},{9,... | collective-permute-start | bytes 184328 | tf_op jit(solution)/shard_map/ppermute | solution.py:112
  66.9 0.7 fusion.68
  67.6 1.5 %collective-permute-start.10 = (bf16[24,1280]{1,0:T(8,128)(2,1)}, bf16[24,1280]{1,0:T(8,128)(2,1)S(1)}, u32[]{:S(2)}, u32[]{:S(2)}) collective-permute-start(bf16[24,1280]{1,0:T(8,128)(2,1)} %get-tuple-element.22), channel_id=1, source_target_pairs={{0,24},{1,25},{2,26},{3,27},{4,28},{5,29},{6,30},{7,31},{8,16},{9,... | collective-permute-start | bytes 184328 | tf_op jit(solution)/shard_map/ppermute | solution.py:112
  69.3 2.7 %collective-permute-start.9 = (bf16[24,1280]{1,0:T(8,128)(2,1)S(1)}, bf16[24,1280]{1,0:T(8,128)(2,1)}, u32[]{:S(2)}, u32[]{:S(2)}) collective-permute-start(bf16[24,1280]{1,0:T(8,128)(2,1)S(1)} %get-tuple-element.23), channel_id=1, source_target_pairs={{0,16},{1,17},{2,18},{3,19},{4,20},{5,21},{6,22},{7,23},{8,24},{9,... | collective-permute-start | bytes 184328 | tf_op jit(solution)/shard_map/ppermute | solution.py:112
  72.0 1.9 %collective-permute-done.10 = bf16[24,1280]{1,0:T(8,128)(2,1)S(1)} collective-permute-done((bf16[24,1280]{1,0:T(8,128)(2,1)}, bf16[24,1280]{1,0:T(8,128)(2,1)S(1)}, u32[]{:S(2)}, u32[]{:S(2)}) %collective-permute-start.10) | collective-permute-done | bytes 61472 | tf_op jit(solution)/shard_map/ppermute | solution.py:112
  74.0 0.6 collective-permute-done.8
  74.6 1.7 %collective-permute-done.9 = bf16[24,1280]{1,0:T(8,128)(2,1)} collective-permute-done((bf16[24,1280]{1,0:T(8,128)(2,1)S(1)}, bf16[24,1280]{1,0:T(8,128)(2,1)}, u32[]{:S(2)}, u32[]{:S(2)}) %collective-permute-start.9) | collective-permute-done | bytes 61472 | tf_op jit(solution)/shard_map/ppermute | solution.py:112
  76.3 0.9 fusion.54
  77.6 2.7 %gather_fusion.1 = bf16[24,4,128,128]{3,2,1,0:T(8,128)(2,1)} fusion(bf16[16,4,128,128]{3,2,1,0:T(8,128)(2,1)S(1)} %copy-done, s32[1024]{0:T(1024)S(1)} %pad_clamp_fusion), kind=kCustom, calls=%fused_computation.1.clone | custom fusion | bytes 6291552 | tf_op jit(solution)/shard_map/jit(_take)/gather | solution.py:35
  80.4 4.3 %gather_fusion = bf16[24,4,128,128]{3,2,1,0:T(8,128)(2,1)} fusion(bf16[16,4,128,128]{3,2,1,0:T(8,128)(2,1)} %param.23, s32[1024]{0:T(1024)S(1)} %pad_clamp_fusion), kind=kCustom, calls=%fused_computation.clone | custom fusion | bytes 6291552 | tf_op jit(solution)/shard_map/jit(_take)/gather | solution.py:36
  86.5 0.6 fusion.99
  87.2 3.4 %bitcast_reduce_fusion = (f32[3,4,4,8]{3,1,2,0:T(4,128)S(1)}, f32[3,4,8,128,4,8]{3,5,4,2,1,0:T(8,128)S(1)}) fusion(bf16[3,8,4,128,128]{4,3,2,1,0:T(8,128)(2,1)} %bitcast.234, pred[3,8]{1,0:T(4,128)(4,1)S(1)} %copy-done.16, pred[3,8,128]{2,1,0:T(8,128)(4,1)S(1)} %copy-done.10, bf16[3,4,4,8,128]{4,3,2,1,0:T(8,128)(2,1)S(1)} %fusion.48), kind=kOutput, calls=%fused_computation.13 | convolution fusion | flops 103415424 | bytes 4821528 | tf_op jit(solution)/shard_map/rtkgd,rmknd->rtkgmn/dot_general | solution.py:38
  90.7 0.4 fusion.16
  91.2 1.0 %fusion.17 = f32[3,4,128,4,8]{2,4,3,1,0:T(8,128)S(1)} fusion(bf16[3,8,4,128,128]{4,3,2,1,0:T(8,128)(2,1)S(1)} %bitcast.233, pred[3,8]{1,0:T(4,128)(4,1)S(1)} %copy-done.16, f32[3,4,8,128,4,8]{3,5,4,2,1,0:T(8,128)S(1)} %get-tuple-element.53, f32[3,4,4,8]{3,1,2,0:T(4,128)S(1)} %add.371, f32[3,4,4,8]{3,1,2,0:T(4,128)S(1)} %max.11, ...), kind=kOutput, calls=%fused_computation.30 | convolution fusion | flops 103809024 | bytes 4921368 | tf_op jit(solution)/shard_map/rtkgmn,rmknd->rtkgd/dot_general | solution.py:55
  92.5 0.7 convert_element_type.210
  (125 shorter events, 4.6 us)
Async XLA Ops:
  0.0 77.6 %copy-start = (bf16[16,4,128,128]{3,2,1,0:T(8,128)(2,1)S(1)}, bf16[16,4,128,128]{3,2,1,0:T(8,128)(2,1)}, u32[]{:S(2)}) copy-start(bf16[16,4,128,128]{3,2,1,0:T(8,128)(2,1)} %param.22) | copy-start | bytes 6291460
  1.2 15.3 %collective-permute-start = (bf16[2,2,2,48,256]{4,2,1,0,3:T(2,128)(2,1)S(1)}, bf16[2,2,2,48,256]{4,2,1,0,3:T(2,128)(2,1)}, u32[]{:S(2)}, u32[]{:S(2)}) collective-permute-start(bf16[2,2,2,48,256]{4,2,1,0,3:T(2,128)(2,1)S(1)} %bitcast.237), channel_id=1, source_target_pairs={{0,0},{1,8},{2,2},{3,10},{4,4},{5,12},{6,6},{7,14},{8,1},{9,9},{10... | collective-permute-start | bytes 589832 | tf_op jit(solution)/shard_map/ppermute | solution.py:112
  3.3 3.7 %copy-start.4 = (f32[256,512]{1,0:T(8,128)S(1)}, f32[256,512]{1,0:T(8,128)}, u32[]{:S(2)}) copy-start(f32[256,512]{1,0:T(8,128)} %param.18) | copy-start | bytes 1572868
  3.3 3.7 %copy-start.5 = (f32[256,512]{1,0:T(8,128)S(1)}, f32[256,512]{1,0:T(8,128)}, u32[]{:S(2)}) copy-start(f32[256,512]{1,0:T(8,128)} %param.17) | copy-start | bytes 1572868
  7.8 5.1 %copy-start.3 = (bf16[12,4,2048]{2,1,0:T(4,128)(2,1)S(1)}, bf16[12,4,2048]{2,1,0:T(4,128)(2,1)}, u32[]{:S(2)}) copy-start(bf16[12,4,2048]{2,1,0:T(4,128)(2,1)} %param.14) | copy-start | bytes 589828
  7.8 5.4 %copy-start.9 = (f32[1024]{0:T(1024)S(1)}, f32[1024]{0:T(1024)}, u32[]{:S(2)}) copy-start(f32[1024]{0:T(1024)} %param.19) | copy-start | bytes 12292
  7.8 5.4 %copy-start.14 = (f32[128]{0:T(128)S(1)}, f32[128]{0:T(128)}, u32[]{:S(2)}) copy-start(f32[128]{0:T(128)} %param.20) | copy-start | bytes 1540
  7.8 5.4 %copy-start.15 = (f32[128]{0:T(128)S(1)}, f32[128]{0:T(128)}, u32[]{:S(2)}) copy-start(f32[128]{0:T(128)} %param.21) | copy-start | bytes 1540
  7.9 7.1 %copy-start.13 = (s32[3]{0:T(128)S(1)}, s32[3]{0:T(128)}, u32[]{:S(2)}) copy-start(s32[3]{0:T(128)} %param.24) | copy-start | bytes 40
  7.9 7.9 %copy-start.11 = (s32[3,8]{1,0:T(4,128)S(1)}, s32[3,8]{1,0:T(4,128)}, u32[]{:S(2)}) copy-start(s32[3,8]{1,0:T(4,128)} %param.25) | copy-start | bytes 292
  9.2 29.5 %collective-permute-start.11 = (bf16[256,1280]{1,0:T(8,128)(2,1)}, bf16[256,1280]{1,0:T(8,128)(2,1)}, u32[]{:S(2)}, u32[]{:S(2)}) collective-permute-start(bf16[256,1280]{1,0:T(8,128)(2,1)} %get-tuple-element.50), channel_id=1, source_target_pairs={{0,1},{1,0},{2,3},{3,2},{4,5},{5,4},{6,7},{7,6},{8,9},{9,8},{10,11... | collective-permute-start | bytes 1966088 | tf_op jit(solution)/shard_map/ppermute | solution.py:112
  13.0 29.4 %collective-permute-start.5 = (bf16[256,1280]{1,0:T(8,128)(2,1)}, bf16[256,1280]{1,0:T(8,128)(2,1)}, u32[]{:S(2)}, u32[]{:S(2)}) collective-permute-start(bf16[256,1280]{1,0:T(8,128)(2,1)} %get-tuple-element.51), channel_id=1, source_target_pairs={{0,1},{1,0},{2,3},{3,2},{4,5},{5,4},{6,7},{7,6},{8,9},{9,8},{10,11... | collective-permute-start | bytes 1966088 | tf_op jit(solution)/shard_map/ppermute | solution.py:112
  13.3 12.1 %collective-permute-start.17 = (f32[1328]{0:T(1024)S(1)}, f32[1328]{0:T(1024)S(1)}, u32[]{:S(2)}, u32[]{:S(2)}) collective-permute-start(f32[1328]{0:T(1024)S(1)} %pad_maximum_fusion.3), channel_id=1, source_target_pairs={{0,2},{1,3},{2,0},{3,1},{4,6},{5,7},{6,4},{7,5},{8,10},{9,11},{10,... | collective-permute-start | bytes 15944 | tf_op jit(solution)/shard_map/ppermute | solution.py:112
  17.5 5.0 %collective-permute-start.1 = (bf16[2,2,48,256]{3,1,0,2:T(2,128)(2,1)S(1)}, bf16[2,2,48,256]{3,1,0,2:T(2,128)(2,1)S(1)}, u32[]{:S(2)}, u32[]{:S(2)}) collective-permute-start(bf16[2,2,48,256]{3,1,0,2:T(2,128)(2,1)S(1)} %dynamic-slice_bitcast_fusion), channel_id=1, source_target_pairs={{0,2},{1,3},{2,0},{3,1},{4,6},{5,7},{6,4},{7,5},{8,10},{9,11},{10,... | collective-permute-start | bytes 294920 | tf_op jit(solution)/shard_map/ppermute | solution.py:112
  23.8 4.7 %collective-permute-start.2 = (bf16[2,2,48,256]{3,2,1,0:T(8,128)(2,1)S(1)}, bf16[2,2,48,256]{3,2,1,0:T(8,128)(2,1)S(1)}, u32[]{:S(2)}, u32[]{:S(2)}) collective-permute-start(bf16[2,2,48,256]{3,2,1,0:T(8,128)(2,1)S(1)} %bitcast.238), channel_id=1, source_target_pairs={{0,4},{1,5},{2,6},{3,7},{4,0},{5,1},{6,2},{7,3},{8,12},{9,13},{10,... | collective-permute-start | bytes 294920 | tf_op jit(solution)/shard_map/ppermute | solution.py:112
  29.2 6.4 %collective-permute-start.3 = (bf16[2,2,48,256]{3,2,0,1:T(8,128)(2,1)}, bf16[2,2,48,256]{3,2,0,1:T(8,128)(2,1)}, u32[]{:S(2)}, u32[]{:S(2)}) collective-permute-start(bf16[2,2,48,256]{3,2,0,1:T(8,128)(2,1)} %fusion.60), channel_id=1, source_target_pairs={{0,16},{1,17},{2,18},{3,19},{4,20},{5,21},{6,22},{7,23},{8,24},{9,... | collective-permute-start | bytes 294920 | tf_op jit(solution)/shard_map/ppermute | solution.py:112
  32.4 5.7 %copy-start.1 = (f32[256,1024]{1,0:T(8,128)S(1)}, f32[256,1024]{1,0:T(8,128)}, u32[]{:S(2)}) copy-start(f32[256,1024]{1,0:T(8,128)} %get-tuple-element.9) | copy-start | bytes 3145732
  32.4 5.7 %copy-start.7 = (f32[256,128]{1,0:T(8,128)S(1)}, f32[256,128]{1,0:T(8,128)}, u32[]{:S(2)}) copy-start(f32[256,128]{1,0:T(8,128)} %get-tuple-element.17) | copy-start | bytes 393220
  32.4 5.7 %copy-start.8 = (f32[256,128]{1,0:T(8,128)S(1)}, f32[256,128]{1,0:T(8,128)}, u32[]{:S(2)}) copy-start(f32[256,128]{1,0:T(8,128)} %get-tuple-element.56) | copy-start | bytes 393220
  36.6 1.5 %collective-permute-start.4 = (bf16[2,2,2,48,256]{4,3,1,0,2:T(8,128)(2,1)S(1)}, bf16[2,2,2,48,256]{4,3,1,0,2:T(8,128)(2,1)S(1)}, u32[]{:S(2)}, u32[]{:S(2)}) collective-permute-start(bf16[2,2,2,48,256]{4,3,1,0,2:T(8,128)(2,1)S(1)} %pad_maximum_fusion), channel_id=1, source_target_pairs={{0,1},{1,0},{2,3},{3,2},{4,5},{5,4},{6,7},{7,6},{8,9},{9,8},{10,11... | collective-permute-start | bytes 589832 | tf_op jit(solution)/shard_map/ppermute | solution.py:112
  38.7 3.2 %copy-start.6 = (f32[256,128]{1,0:T(8,128)S(1)}, f32[256,128]{1,0:T(8,128)}, u32[]{:S(2)}) copy-start(f32[256,128]{1,0:T(8,128)} %get-tuple-element.57) | copy-start | bytes 393220
  40.3 13.3 %collective-permute-start.12 = (bf16[2,2,2,24,1280]{4,3,2,1,0:T(8,128)(2,1)S(1)}, bf16[2,2,2,24,1280]{4,3,2,1,0:T(8,128)(2,1)S(1)}, u32[]{:S(2)}, u32[]{:S(2)}) collective-permute-start(bf16[2,2,2,24,1280]{4,3,2,1,0:T(8,128)(2,1)S(1)} %fusion.39), channel_id=1, source_target_pairs={{0,4},{1,5},{2,6},{3,7},{4,0},{5,1},{6,2},{7,3},{8,12},{9,13},{10,... | collective-permute-start | bytes 1474568 | tf_op jit(solution)/shard_map/ppermute | solution.py:112
  44.0 14.2 %collective-permute-start.6 = (bf16[2,2,2,24,1280]{4,3,2,1,0:T(8,128)(2,1)S(1)}, bf16[2,2,2,24,1280]{4,3,2,1,0:T(8,128)(2,1)S(1)}, u32[]{:S(2)}, u32[]{:S(2)}) collective-permute-start(bf16[2,2,2,24,1280]{4,3,2,1,0:T(8,128)(2,1)S(1)} %fusion.38), channel_id=1, source_target_pairs={{0,2},{1,3},{2,0},{3,1},{4,6},{5,7},{6,4},{7,5},{8,10},{9,11},{10,... | collective-permute-start | bytes 1474568 | tf_op jit(solution)/shard_map/ppermute | solution.py:112
  53.8 8.5 %collective-permute-start.13 = (bf16[2,2,1,24,1280]{4,3,2,1,0:T(8,128)(2,1)S(1)}, bf16[2,2,1,24,1280]{4,3,2,1,0:T(8,128)(2,1)S(1)}, u32[]{:S(2)}, u32[]{:S(2)}) collective-permute-start(bf16[2,2,1,24,1280]{4,3,2,1,0:T(8,128)(2,1)S(1)} %dynamic-slice_convert_fusion), channel_id=1, source_target_pairs={{0,2},{1,3},{2,0},{3,1},{4,6},{5,7},{6,4},{7,5},{8,10},{9,11},{10,... | collective-permute-start | bytes 737288 | tf_op jit(solution)/shard_map/ppermute | solution.py:112
  58.3 8.6 %collective-permute-start.7 = (bf16[2,2,1,24,1280]{4,3,2,1,0:T(8,128)(2,1)S(1)}, bf16[2,2,1,24,1280]{4,3,2,1,0:T(8,128)(2,1)S(1)}, u32[]{:S(2)}, u32[]{:S(2)}) collective-permute-start(bf16[2,2,1,24,1280]{4,3,2,1,0:T(8,128)(2,1)S(1)} %dynamic-slice_convert_fusion.1), channel_id=1, source_target_pairs={{0,4},{1,5},{2,6},{3,7},{4,0},{5,1},{6,2},{7,3},{8,12},{9,13},{10,... | collective-permute-start | bytes 737288 | tf_op jit(solution)/shard_map/ppermute | solution.py:112
  62.4 6.8 %collective-permute-start.14 = (bf16[24,1280]{1,0:T(8,128)(2,1)S(1)}, bf16[24,1280]{1,0:T(8,128)(2,1)S(1)}, u32[]{:S(2)}, u32[]{:S(2)}) collective-permute-start(bf16[24,1280]{1,0:T(8,128)(2,1)S(1)} %get-tuple-element.18), channel_id=1, source_target_pairs={{0,8},{1,9},{2,10},{3,11},{4,12},{5,13},{6,14},{7,15},{8,0},{9,1},... | collective-permute-start | bytes 184328 | tf_op jit(solution)/shard_map/ppermute | solution.py:112
  62.5 9.5 %collective-permute-start.15 = (bf16[24,1280]{1,0:T(8,128)(2,1)S(1)}, bf16[24,1280]{1,0:T(8,128)(2,1)S(1)}, u32[]{:S(2)}, u32[]{:S(2)}) collective-permute-start(bf16[24,1280]{1,0:T(8,128)(2,1)S(1)} %get-tuple-element.20), channel_id=1, source_target_pairs={{0,16},{1,17},{2,18},{3,19},{4,20},{5,21},{6,22},{7,23},{8,24},{9,... | collective-permute-start | bytes 184328 | tf_op jit(solution)/shard_map/ppermute | solution.py:112
  64.6 7.4 %collective-permute-start.16 = (bf16[24,1280]{1,0:T(8,128)(2,1)S(1)}, bf16[24,1280]{1,0:T(8,128)(2,1)S(1)}, u32[]{:S(2)}, u32[]{:S(2)}) collective-permute-start(bf16[24,1280]{1,0:T(8,128)(2,1)S(1)} %get-tuple-element.19), channel_id=1, source_target_pairs={{0,24},{1,25},{2,26},{3,27},{4,28},{5,29},{6,30},{7,31},{8,16},{9,... | collective-permute-start | bytes 184328 | tf_op jit(solution)/shard_map/ppermute | solution.py:112
  67.6 6.4 %collective-permute-start.10 = (bf16[24,1280]{1,0:T(8,128)(2,1)}, bf16[24,1280]{1,0:T(8,128)(2,1)S(1)}, u32[]{:S(2)}, u32[]{:S(2)}) collective-permute-start(bf16[24,1280]{1,0:T(8,128)(2,1)} %get-tuple-element.22), channel_id=1, source_target_pairs={{0,24},{1,25},{2,26},{3,27},{4,28},{5,29},{6,30},{7,31},{8,16},{9,... | collective-permute-start | bytes 184328 | tf_op jit(solution)/shard_map/ppermute | solution.py:112
  69.1 5.5 %collective-permute-start.8 = (bf16[24,1280]{1,0:T(8,128)(2,1)S(1)}, bf16[24,1280]{1,0:T(8,128)(2,1)}, u32[]{:S(2)}, u32[]{:S(2)}) collective-permute-start(bf16[24,1280]{1,0:T(8,128)(2,1)S(1)} %get-tuple-element.21), channel_id=1, source_target_pairs={{0,8},{1,9},{2,10},{3,11},{4,12},{5,13},{6,14},{7,15},{8,0},{9,1},... | collective-permute-start | bytes 184328 | tf_op jit(solution)/shard_map/ppermute | solution.py:112
  69.3 7.0 %collective-permute-start.9 = (bf16[24,1280]{1,0:T(8,128)(2,1)S(1)}, bf16[24,1280]{1,0:T(8,128)(2,1)}, u32[]{:S(2)}, u32[]{:S(2)}) collective-permute-start(bf16[24,1280]{1,0:T(8,128)(2,1)S(1)} %get-tuple-element.23), channel_id=1, source_target_pairs={{0,16},{1,17},{2,18},{3,19},{4,20},{5,21},{6,22},{7,23},{8,24},{9,... | collective-permute-start | bytes 184328 | tf_op jit(solution)/shard_map/ppermute | solution.py:112
  77.5 7.4 %collective-permute-start.18 = (f32[2,14,1280]{2,0,1:T(2,128)S(1)}, f32[2,14,1280]{2,0,1:T(2,128)S(1)}, u32[]{:S(2)}, u32[]{:S(2)}) collective-permute-start(f32[2,14,1280]{2,0,1:T(2,128)S(1)} %pad_maximum_fusion.1), channel_id=1, source_target_pairs={{0,1},{1,0},{2,3},{3,2},{4,5},{5,4},{6,7},{7,6},{8,9},{9,8},{10,11... | collective-permute-start | bytes 430088 | tf_op jit(solution)/shard_map/ppermute | solution.py:112
  80.4 4.4 %copy-start.12 = (f32[48]{0:T(128)S(1)}, f32[48]{0:T(128)}, u32[]{:S(2)}) copy-start(f32[48]{0:T(128)} %get-tuple-element.46) | copy-start | bytes 580
  86.0 1.1 %copy-start.10 = (pred[3,8,128]{2,1,0:T(8,128)(4,1)S(1)}, pred[3,8,128]{2,1,0:T(8,128)(4,1)}, u32[]{:S(2)}) copy-start(pred[3,8,128]{2,1,0:T(8,128)(4,1)} %broadcast_compare_fusion) | copy-start | bytes 9220
  86.0 1.1 %copy-start.16 = (pred[3,8]{1,0:T(4,128)(4,1)S(1)}, pred[3,8]{1,0:T(4,128)(4,1)}, u32[]{:S(2)}) copy-start(pred[3,8]{1,0:T(4,128)(4,1)} %compare_and_fusion) | copy-start | bytes 76
  87.2 4.0 %copy-start.2 = (bf16[24,4,128,128]{3,2,1,0:T(8,128)(2,1)S(1)}, bf16[24,4,128,128]{3,2,1,0:T(8,128)(2,1)}, u32[]{:S(2)}) copy-start(bf16[24,4,128,128]{3,2,1,0:T(8,128)(2,1)} %gather_fusion) | copy-start | bytes 9437188

commit v3 on v2

--- a/solution.py
+++ b/solution.py
@@ -1,6 +1,10 @@
+import functools
+
 import jax
 import jax.numpy as jnp
 from jax import lax
+from jax.experimental import pallas as pl
+from jax.experimental.pallas import tpu as pltpu
 from jax.sharding import PartitionSpec as P
 
 HD = 128
@@ -57,6 +61,122 @@
         "rtkgs,rskd->rtkgd", w_fresh, value_new, preferred_element_type=jnp.float32
     )
     return out.reshape(rows, steps, HQ * HD).astype(jnp.bfloat16)
+
+
+def attend_kernel(heads, len_ref, tab_ref, core_ref, mine, other, scale, bias, cos, sin, keys, vals,
+                  out, q32, qb, kf, vf, score, top, low, acc):
+    slots = keys.shape[0]
+    rows, steps = out.shape[:2]
+    most = tab_ref.shape[1]
+    own = rows * steps
+    group = mine.shape[2] // HD - 2
+    lanes = group * steps
+    fresh = kf.shape[1]
+    core = core_ref[0]
+    ends = []
+    for r in range(rows):
+        ends.append((ends[-1] if ends else 0) + lax.div(len_ref[r] + (PAGE - 1), PAGE))
+    row_of, live_of, page_of = [], [], []
+    for s in range(slots):
+        row, start = jnp.int32(0), jnp.int32(0)
+        for r in range(rows - 1):
+            past = s >= ends[r]
+            row = jnp.where(past, r + 1, row)
+            start = jnp.where(past, ends[r], start)
+        i = s - start
+        page = tab_ref[row, jnp.minimum(i, most - 1)]
+        row_of.append(row)
+        live_of.append(len_ref[row] - i * PAGE)
+        page_of.append(page)
+    kf[...] = jnp.zeros_like(kf)
+    vf[...] = jnp.zeros_like(vf)
+    cosv, sinv, by_row = cos[...], sin[...], scale[...]
+    per = len(heads) // 2
+    for i in range(len(heads)):
+        src = mine if i < per else other
+        at = lambda n: src[i % per, :own, n * HD : (n + 1) * HD] * by_row + bias[i : i + 1, n * HD : (n + 1) * HD]
+        turn = lambda v: v * cosv + pltpu.roll(v, HD // 2, 1) * sinv
+        for n in range(group):
+            v = turn(at(n))
+            for r in range(rows):
+                q32[i, r, n * steps : (n + 1) * steps, :] = v[r * steps : (r + 1) * steps]
+        kf[i, :own, :] = turn(at(group))
+        vf[i, :own, :] = at(group + 1)
+    qb[...] = q32[...].astype(BF)
+    top[...] = jnp.full_like(top, -1e30)
+    factor = 1.0 / HD**0.5
+    nt = (((1,), (1,)), ((), ()))
+    lane = lax.broadcasted_iota(jnp.int32, (lanes, PAGE), 1)
+    flane = lax.broadcasted_iota(jnp.int32, (lanes, fresh), 1)
+    fstep = lax.rem(lax.broadcasted_iota(jnp.int32, (lanes, fresh), 0), steps)
+    for i in range(len(heads)):
+        head = heads[i](core)
+        for s in range(slots):
+            row = row_of[s]
+            v = lax.dot_general(qb[i, row], keys[page_of[s], head], nt, preferred_element_type=F32) * factor
+            v = jnp.where(lane < live_of[s], v, -1e30)
+            score[i, s] = v
+            top[i, row] = jnp.maximum(top[i, row], v)
+        for r in range(rows):
+            v = lax.dot_general(qb[i, r], kf[i].astype(BF), nt, preferred_element_type=F32) * factor
+            ok = (flane >= r * steps) & (flane - r * steps <= fstep)
+            v = jnp.where(ok, v, -1e30)
+            most_v = jnp.maximum(jnp.max(top[i, r], 1, keepdims=True), jnp.max(v, 1, keepdims=True))
+            top[i, r] = jnp.broadcast_to(most_v, (lanes, PAGE))
+            e = jnp.where(ok, jnp.exp(v - most_v), 0.0)
+            low[i, r] = jnp.where(lane == 0, jnp.sum(e, 1, keepdims=True), 0.0)
+            acc[i, r] = jnp.dot(e.astype(BF), vf[i].astype(BF), preferred_element_type=F32)
+        for s in range(slots):
+            row = row_of[s]
+            e = jnp.exp(score[i, s] - top[i, row])
+            low[i, row] = low[i, row] + e
+            acc[i, row] = acc[i, row] + jnp.dot(e.astype(BF), vals[page_of[s], head], preferred_element_type=F32)
+        for r in range(rows):
+            v = (acc[i, r] / jnp.sum(low[i, r], 1, keepdims=True)).astype(BF)
+            for n in range(group):
+                at_col = pl.multiple_of(head * (group * HD), HD) + n * HD
+                out[r, :, pl.ds(pl.multiple_of(at_col, HD), HD)] = v[n * steps : (n + 1) * steps]
+
+
+def attend_paged(core, mine, other, scale, bias, cos, sin, key_pages, value_pages, kv_lengths, page_table):
+    rows = kv_lengths.shape[0]
+    steps = scale.shape[0] // rows
+    group = HQ // KVH
+    slots = key_pages.shape[0]
+    per = KVH // 2
+    heads = [lambda c, g=g: c + 2 * g for g in range(per)] + [lambda c, g=g: 1 - c + 2 * g for g in range(per)]
+    smem = pl.BlockSpec(memory_space=pltpu.SMEM)
+    vmem = pl.BlockSpec(memory_space=pltpu.VMEM)
+    key_pages, value_pages = (pltpu.with_memory_space_constraint(a, pltpu.VMEM) for a in (key_pages, value_pages))
+    part = (KVH, rows, group * steps, HD)
+    own16 = -(-rows * steps // 16) * 16
+    return pl.pallas_call(
+        functools.partial(attend_kernel, heads),
+        out_shape=jax.ShapeDtypeStruct((rows, steps, HQ * HD), BF),
+        in_specs=[smem] * 3 + [vmem] * 8,
+        out_specs=vmem,
+        scratch_shapes=[
+            pltpu.VMEM(part, F32),
+            pltpu.VMEM(part, BF),
+            pltpu.VMEM((KVH, own16, HD), F32),
+            pltpu.VMEM((KVH, own16, HD), F32),
+            pltpu.VMEM((KVH, slots, group * steps, PAGE), F32),
+            pltpu.VMEM(part, F32),
+            pltpu.VMEM(part, F32),
+            pltpu.VMEM(part, F32),
+        ],
+        compiler_params=pltpu.CompilerParams(vmem_limit_bytes=12 << 20),
+        name="attend_paged",
+    )(kv_lengths, page_table, core.reshape(1), mine, other, scale, bias, cos, sin, key_pages, value_pages)
+
+
+def turns(kv_lengths, steps):
+    positions = kv_lengths[:, None] + jnp.arange(steps, dtype=jnp.int32)[None, :]
+    half = HD // 2
+    freq = THETA ** (-(jnp.arange(half, dtype=F32) * 2.0 / HD))
+    angle = positions.reshape(-1).astype(F32)[:, None] * freq
+    cos, sin = jnp.cos(angle), jnp.sin(angle)
+    return jnp.concatenate([cos, cos], 1), jnp.concatenate([-sin, sin], 1)
 
 
 def weights_plan(hidden, norm_gain, w_query, w_key, w_value, bias_query, bias_key, bias_value,
@@ -81,20 +201,59 @@
     return attend(query, key_new, value_new, key_pages, value_pages, kv_lengths, page_table)
 
 
+def cast_kernel(core_ref, wq, wk, wv, own, sib):
+    i = pl.program_id(0)
+    per = pl.num_programs(0) // 2
+
+    def put(out):
+        qw = wq.shape[1]
+        out[0, :, :qw] = wq[...].astype(BF)
+        out[0, :, qw : qw + HD] = wk[...].astype(BF)
+        out[0, :, qw + HD :] = wv[...].astype(BF)
+
+    pl.when(i < per)(lambda: put(own))
+    pl.when(i >= per)(lambda: put(sib))
+
+
+def cast_weights(core, w_query, w_key, w_value):
+    kw, qw, per = w_query.shape[0], HQ // KVH * HD, KVH // 2
+    head = lambda i, c: jnp.where(i < per, c[0] + 2 * i, 1 - c[0] + 2 * (i - per))
+    spec = lambda w: pl.BlockSpec((kw, w), lambda i, c: (0, head(i, c)))
+    shape = jax.ShapeDtypeStruct((per, kw, qw + 2 * HD), BF)
+    block = (1,) + shape.shape[1:]
+    return pl.pallas_call(
+        cast_kernel,
+        out_shape=(shape, shape),
+        grid_spec=pltpu.PrefetchScalarGridSpec(
+            num_scalar_prefetch=1,
+            grid=(2 * per,),
+            in_specs=[spec(qw), spec(HD), spec(HD)],
+            out_specs=[
+                pl.BlockSpec(block, lambda i, c: (jnp.minimum(i, per - 1), 0, 0)),
+                pl.BlockSpec(block, lambda i, c: (jnp.maximum(i - per, 0), 0, 0)),
+            ],
+        ),
+        compiler_params=pltpu.CompilerParams(vmem_limit_bytes=24 << 20),
+        name="cast_weights",
+    )(core.reshape(1), w_query, w_key, w_value)
+
+
+def after(a, *others):
+    return lax.optimization_barrier((a,) + others)[0]
+
+
 def sums_plan(R, T, hidden, norm_gain, w_query, w_key, w_value, bias_query, bias_key, bias_value,
               key_pages, value_pages, kv_lengths, page_table):
     ri, ti = lax.axis_index("replica"), lax.axis_index("tp")
-    me = ri * T + ti
     y, z, c, x = ri % 2, ri // 2, ti % 2, ti // 2
-    Z = R // 2
-    count, steps, _ = hidden.shape
+    zh, zl = z // 2, z % 2
+    count, steps, width = hidden.shape
     kw = w_query.shape[0]
     D = norm_gain.shape[0]
     rows = count // T
     own = rows * steps
     G = KVH // 2
-    qw = HQ // KVH * HD
-    gw = qw + 2 * HD
+    gw = HQ // KVH * HD + 2 * HD
 
     def perm(f):
         pairs = []
@@ -104,82 +263,70 @@
             pairs.append((i, (zz * 2 + yy) * T + xx * 2 + cc))
         return pairs
 
-    to_core = perm(lambda z, y, x, c: (z, y, x, 1 - c))
-    to_x = perm(lambda z, y, x, c: (z, y, 1 - x, c))
-    to_y = perm(lambda z, y, x, c: (z, 1 - y, x, c))
+    def flip(dz=0, dy=0, dx=0, dc=0):
+        return perm(lambda z, y, x, c: (z ^ dz, y ^ dy, x ^ dx, c ^ dc))
 
     def send(a, pairs):
         return lax.ppermute(a, AXES, pairs)
 
     pick = lambda a, i, axis=0: lax.dynamic_index_in_dim(a, i, axis, keepdims=False)
 
-    def both(i, mine, other):
-        return jnp.stack([jnp.where(i == 0, mine, other), jnp.where(i == 0, other, mine)])
-
-    zh, zl = z // 2, z % 2
-    acts = hidden.reshape(T * own, 2, 2, 2, kw).transpose(1, 2, 3, 0, 4)
+    gain = lax.dynamic_slice_in_dim(norm_gain, ti * width, width)
+    acts = (hidden.astype(F32) * gain).astype(BF).reshape(T * own, 2, 2, 2 * kw).transpose(1, 2, 0, 3)
+    start = acts
     acts = send(acts, perm(lambda z, y, x, c: (z // 2 * 2 + c, y, x, z % 2)))
-    acts = both(x, pick(acts, x, 1), send(pick(acts, 1 - x, 1), to_x))
-    acts = both(y, pick(acts, y, 1), send(pick(acts, 1 - y, 1), to_y))
-    to_far = perm(lambda z, y, x, c: (z ^ 2, y, x, c))
-    acts = both(zh, pick(acts, zh, 1), send(pick(acts, 1 - zh, 1), to_far))
-    acts = both(c, acts, send(acts, to_core))
-    acts_own, acts_sib = pick(acts, c, 3), pick(acts, 1 - c, 3)
-
-    gain = lax.dynamic_slice_in_dim(norm_gain, me * kw, kw)[:, None]
-
-    def columns(cc, g):
-        h = cc + 2 * g
-        parts = [
-            lax.dynamic_slice_in_dim(w_query, h * qw, qw, 1),
-            lax.dynamic_slice_in_dim(w_key, h * HD, HD, 1),
-            lax.dynamic_slice_in_dim(w_value, h * HD, HD, 1),
-        ]
-        return (jnp.concatenate(parts, 1) * gain).astype(BF)
-
-    w_own = [columns(c, g) for g in range(G)]
-    w_sib = [send(columns(1 - c, g), to_core) for g in range(G)]
-
-    wide = hidden.astype(F32)
-    power = jnp.sum(wide * wide, axis=2).reshape(T * own)
+    there = acts
+    at = lambda dy, dx: pick(pick(acts, y ^ dy), x ^ dx)
+    block = lambda dy, dx: send(at(dy, dx), flip(dy=dy, dx=dx)) if dy or dx else at(0, 0)
+    acts = jnp.stack([jnp.stack([block(0, dx), block(1, dx)]) for dx in range(2)])
+    far = pick(acts, 1 ^ zh ^ x)
+    acts = jnp.stack([pick(acts, zh ^ x), send(far, flip(dz=2))])
+    acts = jnp.stack([acts, send(acts, flip(dc=1))])
+
+    w_own, w_sib = cast_weights(after(c, start), w_query, w_key, w_value)
+    w_sib = send(after(w_sib, there), flip(dc=1))
+
+    late = after(hidden, there).astype(F32)
+    power = jnp.sum(late * late, axis=2).reshape(T * own)
     bias = jnp.concatenate([bias_query, bias_key, bias_value])
-    there = send(jnp.concatenate([bias, power]), to_x)
-    biases = both(x, bias, there[:gw])
-    power = power + there[gw:]
-
-    def dot(g):
-        f = lambda a, w: jnp.einsum("abymk,kn->abymn", a, w, preferred_element_type=F32)
-        out = f(acts_own, w_own[g]) + f(acts_sib, w_sib[g])
-        return out.reshape(2, 2, 2, 2, 2 * own, gw)
-
-    done = []
+    got = send(jnp.concatenate([bias, power]), flip(dx=1))
+    biases = jnp.stack([jnp.where(x == 0, bias, got[:gw]), jnp.where(x == 0, got[:gw], bias)])
+    power = power + got[gw:]
+    got = send(jnp.concatenate([biases.reshape(-1), power]), flip(dc=1))
+    biases = jnp.concatenate([biases, got[: G * gw].reshape(G, gw)])
+    power = pick((power + got[G * gw :]).reshape(T, own), ti)
+    row_scale = jnp.broadcast_to(lax.rsqrt(power / D + EPS)[:, None], (own, HD))
+    cos, sin = turns(after(kv_lengths, there), steps)
+
+    def dot(a, g):
+        f = lambda i, w: jnp.einsum("abymk,kn->abymn", pick(a.reshape(a.shape[:-1] + (2, kw)), i, 4), w[g],
+                                    preferred_element_type=F32)
+        return f(c, w_own) + f(1 - c, w_sib)
+
+    half = lambda a, i: pick(a.reshape(a.shape[:3] + (2, 2 * own, a.shape[-1])), i, 3)
+    to_x, to_y = flip(dx=1), flip(dy=1)
+    parts = []
     for g in range(G):
-        part = dot(g)
-        for i, axis, pairs in ((x, 3, to_x), (y, 2, to_y))[:: 1 if g % 2 == 0 else -1]:
-            there = send(pick(part, 1 - i, axis).astype(BF), pairs)
-            part = jnp.expand_dims(pick(part, i, axis) + there.astype(F32), axis)
-        part = part.reshape(2, 2, 2 * own, gw)
-        at = lambda z: pick(pick(part, z % 2), z // 2)
-        total = at(z)
-        for k in range(1, Z):
-            pairs = perm(lambda z, y, x, c: (z ^ k, y, x, c))
-            total = total + send(at(z ^ k).astype(BF), pairs).astype(F32)
-        done.append(total.reshape(2, own, gw))
-    done = jnp.stack(done)
-    mine, other = pick(done, c, 1), pick(done, 1 - c, 1)
-    low = jnp.pad(power, (0, G * gw - T * own)).reshape(G, 1, gw)
-    other = send(jnp.concatenate([other, biases[:, None], low], 1), to_core)
-    full = both(c, mine, other[:, :own]).transpose(1, 0, 2, 3).reshape(KVH, own, gw)
-    bias_all = both(c, biases, other[:, own]).transpose(1, 0, 2).reshape(KVH, gw)
-    power = power + other[:, own + 1].reshape(-1)[: T * own]
-    row_scale = lax.rsqrt(pick(power.reshape(T, own), ti) / D + EPS)
-    full = full * row_scale[None, :, None] + bias_all[:, None, :]
-    full = full.astype(BF).reshape(KVH, rows, steps, gw)
-    query = full[..., :qw].reshape(KVH, rows, steps, HQ // KVH, HD).transpose(1, 2, 0, 3, 4)
-    query = query.reshape(rows, steps, HQ, HD)
-    key_new = full[..., qw : qw + HD].transpose(1, 2, 0, 3)
-    value_new = full[..., qw + HD :].transpose(1, 2, 0, 3)
-    return attend(query, key_new, value_new, key_pages, value_pages, kv_lengths, page_table)
+        if g % 2 == 0:
+            got = send(dot(half(acts, 1 - x), g).astype(BF), to_x)
+            part = dot(half(acts, x), g) + got
+            part = part[:, :, 0] + send(part[:, :, 1].astype(BF), to_y)
+        else:
+            got = send(dot(acts[:, :, 1:], g).astype(BF), to_y)
+            part = dot(acts[:, :, :1], g) + got
+            got = send(half(part, 1 - x)[:, :, 0].astype(BF), to_x)
+            part = half(part, x)[:, :, 0] + got
+        parts.append(part)
+    parts = jnp.stack(parts, 2)
+    at = lambda k: pick(parts[:, k // 2], zl ^ c ^ (k % 2))
+    total = at(0)
+    for k in range(1, R // 2):
+        total = total + send(at(k).astype(BF), flip(dz=k))
+    total = total.reshape(G, 2, own, gw)
+    mine, other = pick(total, c, 1), send(pick(total, 1 - c, 1), flip(dc=1))
+    return attend_paged(
+        c, mine, other, row_scale, biases, cos, sin, key_pages, value_pages, kv_lengths, page_table
+    )
 
 
 def solution(mesh):

time: 93.6 us -> 78.5 us (0.84)
  local copies, waits for them, and re-layouts: 17.3 us -> 9.04 us
  Pallas kernels: 0 us -> 5.3 us
  other arithmetic: 9.28 us -> 4.56 us
  waiting for transfers between devices: 33.1 us -> 28.5 us
  matrix products: 9.33 us -> 6.72 us
    gather x2 -> x0, local copies, waits for them, and re-layouts: 7.02 us -> none  [the longest x1 4.27 us: attend(): vals = jnp.take(value_pages, page_table, axis=0)]
    pallas_call x0 -> x2, Pallas kernels: none -> 5.3 us  [the longest x1 4.4 us: attend_paged(): pl.pallas_call(functools.partial(attend_kernel, heads), out_shape=jax.Sha...]
    ppermute x19 -> x17, waiting for transfers between devices: 33.1 us -> 28.5 us  [send(): return lax.ppermute(a, AXES, pairs)]
    dynamic_slice x3 -> x1, local copies, waits for them, and re-layouts: 5.29 us -> 0.79 us  [sums_plan(): gain = lax.dynamic_slice_in_dim(norm_gain, ti * width, width)]
    unnamed x37 -> x32, local copies, waits for them, and re-layouts: 0.09 us -> 4.07 us
    dot_general x8, matrix products: 9.33 us -> 6.72 us  [dot(): jnp.einsum('abymk,kn->abymn', pick(a.reshape(a.shape[:-1] + (2, kw)), i,...]
    dynamic_slice x3 -> x9, local copies, waits for them, and re-layouts: 0.14 us -> 2.19 us  [sums_plan(): lax.dynamic_index_in_dim(a, i, axis, keepdims=False)]
    convert_element_type x10 -> x4, local copies, waits for them, and re-layouts: 1.67 us -> 0.17 us  [the longest x1 0.08 us: turns(): angle = positions.reshape(-1).astype(F32)[:, None] * freq]
  transfers between devices with their start and end apart: 19 -> 17, of which waited for: 10 -> 10; matrix products, arithmetic and copies ran while one was open for 27% -> 16% of each run, Pallas kernels for 0% -> 1%
where the time goes in v3:
time: 78.5 us; the launch traced here: 78 us
  waiting for transfers between devices  28.5 us (36%)
  starting transfers between devices  23.3 us (30%)
  local copies, waits for them, and re-layouts  9.04 us (12%)
  matrix products  6.72 us (9%)
  Pallas kernels  5.3 us (7%)
  other arithmetic  4.56 us (6%)
    ppermute x17, waiting for transfers between devices, send(): return lax.ppermute(a, AXES, pairs)  28.5 us
    ppermute x17, starting transfers between devices, send(): return lax.ppermute(a, AXES, pairs)  23.3 us
    dot_general x8, matrix products, dot(): jnp.einsum('abymk,kn->abymn', pick(a.reshape(a.shape[:-1] + (2, kw)), i,...  6.72 us
    pallas_call x1, Pallas kernels, attend_paged(): pl.pallas_call(functools.partial(attend_kernel, heads), out_shape=jax.Sha...  4.4 us
    unnamed x32, local copies, waits for them, and re-layouts  4.07 us
    another operation x2, other arithmetic, sums_plan(): acts = jnp.stack([acts, send(acts, flip(dc=1))])  2.63 us
    dynamic_slice x9, local copies, waits for them, and re-layouts, sums_plan(): lax.dynamic_index_in_dim(a, i, axis, keepdims=False)  2.19 us
  transfers between devices with their start and end apart: 17, of which 10 were waited for; matrix products, arithmetic and copies ran while one was open for 16% of the time, Pallas kernels for 1%

profile of v3, /device:TPU:0, one launch (start us, length us, event | category | flops | bytes accessed | tf_op | source)
XLA Modules:
  0.0 78.0 jit_solution(8295608952221039281)
XLA Ops:
  0.0 0.8 %dynamic_slice.93 = f32[2048]{0:T(1024)S(1)} dynamic-slice(f32[8192]{0:T(1024)} %param.13, s32[]{:T(128)S(6)} %select_n.111), dynamic_slice_sizes={2048} | dynamic-slice | bytes 16388 | tf_op jit(solution)/shard_map/dynamic_slice | solution.py:274
  0.8 1.0 %multiply_convert_fusion = bf16[12,4,2048]{2,1,0:T(4,128)(2,1)S(1)} fusion(bf16[12,4,2048]{2,1,0:T(4,128)(2,1)} %param.12, f32[2048]{0:T(1024)S(1)} %dynamic_slice.93), kind=kLoop, calls=%fused_computation.42 | loop fusion | flops 294912 | bytes 401408 | tf_op jit(solution)/shard_map/convert_element_type | solution.py:275
  1.9 0.7 collective-permute-start
  2.8 0.7 constant_dynamic-update-slice_fusion.2
  3.5 2.2 %copy-done = f32[256,4096]{1,0:T(8,128)S(1)} copy-done((f32[256,4096]{1,0:T(8,128)S(1)}, f32[256,4096]{1,0:T(8,128)}, u32[]{:S(2)}) %copy-start) | copy-done | bytes 4194328
  5.7 0.9 %cast_weights.1 = (bf16[2,256,1280]{2,1,0:T(8,128)(2,1)S(1)}, bf16[2,256,1280]{2,1,0:T(8,128)(2,1)S(1)}) custom-call(s32[1]{0:T(128)} %bitcast.12.core_ref, f32[256,4096]{1,0:T(8,128)S(1)} %copy-done, f32[256,512]{1,0:T(8,128)S(1)} %copy-done.3, f32[256,512]{1,0:T(8,128)S(1)} %copy-done.4), custom_call_target="tpu_custom_call" | custom-call | tf_op jit(solution)/shard_map/cast_weights/pallas_call | solution.py:224
  6.6 1.1 %copy-done.7 = bf16[2,256,1280]{2,1,0:T(8,128)(2,1)} copy-done((bf16[2,256,1280]{2,1,0:T(8,128)(2,1)}, bf16[2,256,1280]{2,1,0:T(8,128)(2,1)S(1)}, u32[]{:S(2)}) %copy-start.7) | copy-done | bytes 1310744
  7.7 0.4 constant_dynamic-slice_fusion.14
  8.2 3.0 %collective-permute-start.2 = (bf16[48,512]{1,0:T(8,128)(2,1)S(1)}, bf16[48,512]{1,0:T(8,128)(2,1)S(1)}, u32[]{:S(2)}, u32[]{:S(2)}) collective-permute-start(bf16[48,512]{1,0:T(8,128)(2,1)S(1)} %bitcast.173), channel_id=1, source_target_pairs={{0,2},{1,3},{2,0},{3,1},{4,6},{5,7},{6,4},{7,5},{8,10},{9,11},{10,... | collective-permute-start | bytes 147464 | tf_op jit(solution)/shard_map/ppermute | solution.py:270
  11.2 1.6 %collective-permute-start.3 = (bf16[48,512]{1,0:T(8,128)(2,1)S(1)}, bf16[48,512]{1,0:T(8,128)(2,1)S(1)}, u32[]{:S(2)}, u32[]{:S(2)}) collective-permute-start(bf16[48,512]{1,0:T(8,128)(2,1)S(1)} %bitcast.177), channel_id=1, source_target_pairs={{0,6},{1,7},{2,4},{3,5},{4,2},{5,3},{6,0},{7,1},{8,14},{9,15},{10,... | collective-permute-start | bytes 147464 | tf_op jit(solution)/shard_map/ppermute | solution.py:270
  12.9 0.2 multiply_reduce_fusion
  13.2 2.0 %collective-permute-start.15 = (f32[1328]{0:T(1024)S(1)}, f32[1328]{0:T(1024)S(1)}, u32[]{:S(2)}, u32[]{:S(2)}) collective-permute-start(f32[1328]{0:T(1024)S(1)} %pad_maximum_fusion.6), channel_id=1, source_target_pairs={{0,2},{1,3},{2,0},{3,1},{4,6},{5,7},{6,4},{7,5},{8,10},{9,11},{10,... | collective-permute-start | bytes 15944 | tf_op jit(solution)/shard_map/ppermute | solution.py:270
  15.5 1.4 %collective-permute-done.15 = f32[1328]{0:T(1024)S(1)} collective-permute-done((f32[1328]{0:T(1024)S(1)}, f32[1328]{0:T(1024)S(1)}, u32[]{:S(2)}, u32[]{:S(2)}) %collective-permute-start.15) | collective-permute-done | bytes 5344 | tf_op jit(solution)/shard_map/ppermute | solution.py:270
  17.2 3.1 %collective-permute-start.4 = (bf16[2,48,512]{2,1,0:T(8,128)(2,1)S(1)}, bf16[2,48,512]{2,1,0:T(8,128)(2,1)S(1)}, u32[]{:S(2)}, u32[]{:S(2)}) collective-permute-start(bf16[2,48,512]{2,1,0:T(8,128)(2,1)S(1)} %get-tuple-element.36), channel_id=1, source_target_pairs={{0,16},{1,17},{2,18},{3,19},{4,20},{5,21},{6,22},{7,23},{8,24},{9,... | collective-permute-start | bytes 294920 | tf_op jit(solution)/shard_map/ppermute | solution.py:270
  20.3 3.3 %collective-permute-done.4 = bf16[2,48,512]{2,1,0:T(8,128)(2,1)S(1)} collective-permute-done((bf16[2,48,512]{2,1,0:T(8,128)(2,1)S(1)}, bf16[2,48,512]{2,1,0:T(8,128)(2,1)S(1)}, u32[]{:S(2)}, u32[]{:S(2)}) %collective-permute-start.4) | collective-permute-done | bytes 98336 | tf_op jit(solution)/shard_map/ppermute | solution.py:270
  23.7 0.2 collective-permute-start.5
  23.9 0.4 collective-permute-start.16
  24.4 0.1 collective-permute-start.6
  24.6 0.7 collective-permute-done.16
  25.4 1.0 %pad_maximum_fusion = bf16[2,2,2,2,24,512]{5,4,3,2,1,0:T(8,128)(2,1)S(1)} fusion(bf16[1,2,2,2,24,512]{5,4,3,2,1,0:T(8,128)(2,1)} %bitcast.11, bf16[1,1,2,2,24,512]{5,4,3,2,1,0:T(8,128)(2,1)S(1)} %bitcast.168, bf16[1,1,2,2,24,512]{5,4,3,2,1,0:T(8,128)(2,1)S(1)} %bitcast.166), kind=kLoop, calls=%fused_computation.38 | loop fusion | flops 393216 | bytes 786432 | tf_op jit(solution)/shard_map/stack | solution.py:284
  26.5 1.7 %pad_maximum_fusion.1 = (bf16[2,2,1,48,512]{4,3,2,1,0:T(8,128)(2,1)S(1)}, bf16[2,2,1,48,512]{4,3,2,1,0:T(8,128)(2,1)}) fusion(bf16[1,2,2,48,512]{4,3,2,1,0:T(8,128)(2,1)} %bitcast.27, bf16[1,2,2,48,512]{4,3,2,1,0:T(8,128)(2,1)S(1)} %get-tuple-element.34), kind=kLoop, calls=%fused_computation.59 | loop fusion | flops 196608 | bytes 786432 | tf_op jit(solution)/shard_map/stack | solution.py:284
  28.3 1.0 %reshape.143 = bf16[2,2,1,48,2,256]{5,4,3,1,0,2:T(2,128)(2,1)S(1)} reshape(bf16[2,2,1,48,512]{4,3,2,1,0:T(8,128)(2,1)} %get-tuple-element.22) | data formatting | bytes 393216 | tf_op jit(solution)/shard_map/reshape | solution.py:302
  29.2 0.4 constant_dynamic-slice_fusion.7
  29.7 0.4 constant_dynamic-slice_fusion.10
  30.1 0.4 constant_dynamic-slice_fusion.3
  30.5 0.3 fusion.10
  30.8 0.3 fusion.12
  31.1 0.3 fusion.6
  31.4 1.4 %fusion.3 = bf16[2,2,2,24,1280]{4,3,2,1,0:T(8,128)(2,1)S(1)} fusion(f32[2,2,2,24,1280]{4,3,2,1,0:T(8,128)S(1)} %fusion.10, bf16[2,256,1280]{2,1,0:T(8,128)(2,1)} %collective-permute-done.6, bf16[2,2,2,24,1,256]{5,4,3,2,1,0:T(2,128)(2,1)S(1)} %get-tuple-element.27), kind=kOutput, calls=%fused_computation.7 | convolution fusion | flops 126320640 | bytes 2228224 | tf_op jit(solution)/shard_map/abymk,kn->abymn/dot_general | solution.py:302
  32.8 2.1 %collective-permute-start.7 = (bf16[2,2,2,24,1280]{4,3,2,1,0:T(8,128)(2,1)S(1)}, bf16[2,2,2,24,1280]{4,3,2,1,0:T(8,128)(2,1)S(1)}, u32[]{:S(2)}, u32[]{:S(2)}) collective-permute-start(bf16[2,2,2,24,1280]{4,3,2,1,0:T(8,128)(2,1)S(1)} %fusion.3), channel_id=1, source_target_pairs={{0,2},{1,3},{2,0},{3,1},{4,6},{5,7},{6,4},{7,5},{8,10},{9,11},{10,... | collective-permute-start | bytes 1474568 | tf_op jit(solution)/shard_map/ppermute | solution.py:270
  35.0 0.4 constant_dynamic-slice_fusion.5
  35.4 0.3 fusion.8
  35.7 1.4 %fusion.5 = bf16[2,2,1,48,1280]{4,3,1,0,2:T(8,128)(2,1)S(1)} fusion(f32[2,2,48,1280]{3,2,1,0:T(8,128)S(1)} %fusion.6, bf16[2,256,1280]{2,1,0:T(8,128)(2,1)} %collective-permute-done.6, bf16[2,2,1,48,1,256]{5,4,3,1,0,2:T(2,128)(2,1)S(1)} %get-tuple-element.31), kind=kOutput, calls=%fused_computation.9 | convolution fusion | flops 126320640 | bytes 2228224 | tf_op jit(solution)/shard_map/abymk,kn->abymn/dot_general | solution.py:302
  37.1 1.6 %collective-permute-start.9 = (bf16[2,2,1,48,1280]{4,3,1,0,2:T(8,128)(2,1)S(1)}, bf16[2,2,1,48,1280]{4,3,1,0,2:T(8,128)(2,1)S(1)}, u32[]{:S(2)}, u32[]{:S(2)}) collective-permute-start(bf16[2,2,1,48,1280]{4,3,1,0,2:T(8,128)(2,1)S(1)} %fusion.5), channel_id=1, source_target_pairs={{0,4},{1,5},{2,6},{3,7},{4,0},{5,1},{6,2},{7,3},{8,12},{9,13},{10,... | collective-permute-start | bytes 1474568 | tf_op jit(solution)/shard_map/ppermute | solution.py:270
  38.7 7.8 %collective-permute-done.7 = bf16[2,2,2,24,1280]{4,3,2,1,0:T(8,128)(2,1)S(1)} collective-permute-done((bf16[2,2,2,24,1280]{4,3,2,1,0:T(8,128)(2,1)S(1)}, bf16[2,2,2,24,1280]{4,3,2,1,0:T(8,128)(2,1)S(1)}, u32[]{:S(2)}, u32[]{:S(2)}) %collective-permute-start.7) | collective-permute-done | bytes 491552 | tf_op jit(solution)/shard_map/ppermute | solution.py:270
  46.5 1.4 %fusion = f32[2,2,2,24,1280]{4,3,2,1,0:T(8,128)S(1)} fusion(f32[2,2,2,24,1280]{4,3,2,1,0:T(8,128)S(1)} %fusion.12, bf16[2,2,2,24,1280]{4,3,2,1,0:T(8,128)(2,1)S(1)} %collective-permute-done.7, bf16[2,256,1280]{2,1,0:T(8,128)(2,1)} %collective-permute-done.6, bf16[2,2,2,24,1,256]{5,4,3,2,1,0:T(2,128)(2,1)S(1)} %get-tuple-element.25), kind=kOutput, calls=%fused_computation.4 | convolution fusion | flops 126566400 | bytes 3211264 | tf_op jit(solution)/shard_map/abymk,kn->abymn/dot_general | solution.py:302
  47.9 1.8 %collective-permute-start.8 = (bf16[2,2,24,1280]{3,2,1,0:T(8,128)(2,1)S(1)}, bf16[2,2,24,1280]{3,2,1,0:T(8,128)(2,1)S(1)}, u32[]{:S(2)}, u32[]{:S(2)}) collective-permute-start(bf16[2,2,24,1280]{3,2,1,0:T(8,128)(2,1)S(1)} %fusion.28), channel_id=1, source_target_pairs={{0,4},{1,5},{2,6},{3,7},{4,0},{5,1},{6,2},{7,3},{8,12},{9,13},{10,... | collective-permute-start | bytes 737288 | tf_op jit(solution)/shard_map/ppermute | solution.py:270
  49.8 0.4 collective-permute-done.9
  50.1 1.4 %fusion.2 = f32[2,2,1,48,1280]{4,3,1,0,2:T(8,128)S(1)} fusion(f32[2,2,48,1280]{3,2,1,0:T(8,128)S(1)} %fusion.8, bf16[2,2,1,48,1280]{4,3,1,0,2:T(8,128)(2,1)S(1)} %collective-permute-done.9, bf16[2,256,1280]{2,1,0:T(8,128)(2,1)} %collective-permute-done.6, bf16[2,2,1,48,1,256]{5,4,3,1,0,2:T(2,128)(2,1)S(1)} %get-tuple-element.29), kind=kOutput, calls=%fused_computation.6 | convolution fusion | flops 126566400 | bytes 3211264 | tf_op jit(solution)/shard_map/abymk,kn->abymn/dot_general | solution.py:302
  51.6 1.2 %collective-permute-start.10 = (bf16[2,2,24,1280]{3,2,1,0:T(8,128)(2,1)S(1)}, bf16[2,2,24,1280]{3,2,1,0:T(8,128)(2,1)S(1)}, u32[]{:S(2)}, u32[]{:S(2)}) collective-permute-start(bf16[2,2,24,1280]{3,2,1,0:T(8,128)(2,1)S(1)} %fusion.27), channel_id=1, source_target_pairs={{0,2},{1,3},{2,0},{3,1},{4,6},{5,7},{6,4},{7,5},{8,10},{9,11},{10,... | collective-permute-start | bytes 737288 | tf_op jit(solution)/shard_map/ppermute | solution.py:270
  52.8 2.7 %collective-permute-done.8 = bf16[2,2,24,1280]{3,2,1,0:T(8,128)(2,1)S(1)} collective-permute-done((bf16[2,2,24,1280]{3,2,1,0:T(8,128)(2,1)S(1)}, bf16[2,2,24,1280]{3,2,1,0:T(8,128)(2,1)S(1)}, u32[]{:S(2)}, u32[]{:S(2)}) %collective-permute-start.8) | collective-permute-done | bytes 245792 | tf_op jit(solution)/shard_map/ppermute | solution.py:270
  55.5 3.0 %collective-permute-done.10 = bf16[2,2,24,1280]{3,2,1,0:T(8,128)(2,1)S(1)} collective-permute-done((bf16[2,2,24,1280]{3,2,1,0:T(8,128)(2,1)S(1)}, bf16[2,2,24,1280]{3,2,1,0:T(8,128)(2,1)S(1)}, u32[]{:S(2)}, u32[]{:S(2)}) %collective-permute-start.10) | collective-permute-done | bytes 245792 | tf_op jit(solution)/shard_map/ppermute | solution.py:270
  58.6 1.9 %collective-permute-start.11 = (bf16[2,24,1280]{2,1,0:T(8,128)(2,1)S(1)}, bf16[2,24,1280]{2,1,0:T(8,128)(2,1)S(1)}, u32[]{:S(2)}, u32[]{:S(2)}) collective-permute-start(bf16[2,24,1280]{2,1,0:T(8,128)(2,1)S(1)} %fusion.32), channel_id=1, source_target_pairs={{0,8},{1,9},{2,10},{3,11},{4,12},{5,13},{6,14},{7,15},{8,0},{9,1},... | collective-permute-start | bytes 368648 | tf_op jit(solution)/shard_map/ppermute | solution.py:270
  60.5 3.4 %collective-permute-start.12 = (bf16[2,24,1280]{2,1,0:T(8,128)(2,1)S(1)}, bf16[2,24,1280]{2,1,0:T(8,128)(2,1)S(1)}, u32[]{:S(2)}, u32[]{:S(2)}) collective-permute-start(bf16[2,24,1280]{2,1,0:T(8,128)(2,1)S(1)} %get-tuple-element.17), channel_id=1, source_target_pairs={{0,16},{1,17},{2,18},{3,19},{4,20},{5,21},{6,22},{7,23},{8,24},{9,... | collective-permute-start | bytes 368648 | tf_op jit(solution)/shard_map/ppermute | solution.py:270
  63.9 0.6 collective-permute-done.11
  64.6 7.2 %collective-permute-done.12 = bf16[2,24,1280]{2,1,0:T(8,128)(2,1)S(1)} collective-permute-done((bf16[2,24,1280]{2,1,0:T(8,128)(2,1)S(1)}, bf16[2,24,1280]{2,1,0:T(8,128)(2,1)S(1)}, u32[]{:S(2)}, u32[]{:S(2)}) %collective-permute-start.12) | collective-permute-done | bytes 122912 | tf_op jit(solution)/shard_map/ppermute | solution.py:270
  72.2 1.3 %collective-permute-done.14.other = f32[2,12,1280]{2,1,0:T(8,128)S(1)} collective-permute-done((f32[2,12,1280]{2,1,0:T(8,128)S(1)}, f32[2,12,1280]{2,1,0:T(8,128)S(1)}, u32[]{:S(2)}, u32[]{:S(2)}) %collective-permute-start.14) | collective-permute-done | bytes 122912 | tf_op jit(solution)/shard_map/ppermute | solution.py:270
  73.6 4.4 %attend_paged.1 = bf16[3,4,4096]{2,1,0:T(4,128)(2,1)} custom-call(s32[3]{0:T(128)S(1)} %copy-done.6, s32[3,8]{1,0:T(4,128)S(1)} %copy-done.5, s32[1]{0:T(128)} %bitcast.core_ref, f32[2,12,1280]{2,1,0:T(8,128)S(1)} %bitcast.162, f32[2,12,1280]{2,1,0:T(8,128)S(1)} %collective-permute-done.14.other, f32[12,128]{1,0:T(8,128)S(1)} %broadcast_in_dim.2.scale, ...), custom_call_target="tpu_custom_call" | custom-call | tf_op jit(solution)/shard_map/attend_paged/pallas_call | solution.py:153
  (84 shorter events, 2.2 us)
Async XLA Ops:
  0.0 3.5 %copy-start.3 = (f32[256,512]{1,0:T(8,128)S(1)}, f32[256,512]{1,0:T(8,128)}, u32[]{:S(2)}) copy-start(f32[256,512]{1,0:T(8,128)} %wk.1) | copy-start | bytes 1572868
  0.0 3.5 %copy-start.4 = (f32[256,512]{1,0:T(8,128)S(1)}, f32[256,512]{1,0:T(8,128)}, u32[]{:S(2)}) copy-start(f32[256,512]{1,0:T(8,128)} %wv.1) | copy-start | bytes 1572868
  1.9 5.8 %collective-permute-start = (bf16[2,2,48,512]{3,1,0,2:T(2,128)(2,1)S(1)}, bf16[2,2,48,512]{3,1,0,2:T(2,128)(2,1)S(1)}, u32[]{:S(2)}, u32[]{:S(2)}) collective-permute-start(bf16[2,2,48,512]{3,1,0,2:T(2,128)(2,1)S(1)} %bitcast.169), channel_id=1, source_target_pairs={{0,0},{1,8},{2,2},{3,10},{4,4},{5,12},{6,6},{7,14},{8,1},{9,9},{10... | collective-permute-start | bytes 589832 | tf_op jit(solution)/shard_map/ppermute | solution.py:270
  3.5 2.2 %copy-start = (f32[256,4096]{1,0:T(8,128)S(1)}, f32[256,4096]{1,0:T(8,128)}, u32[]{:S(2)}) copy-start(f32[256,4096]{1,0:T(8,128)} %wq.1) | copy-start | bytes 12582916
  5.7 2.0 %copy-start.12 = (f32[128]{0:T(128)S(1)}, f32[128]{0:T(128)}, u32[]{:S(2)}) copy-start(f32[128]{0:T(128)} %param.18) | copy-start | bytes 1540
  5.7 2.0 %copy-start.11 = (f32[128]{0:T(128)S(1)}, f32[128]{0:T(128)}, u32[]{:S(2)}) copy-start(f32[128]{0:T(128)} %param.19) | copy-start | bytes 1540
  6.6 1.1 %copy-start.7 = (bf16[2,256,1280]{2,1,0:T(8,128)(2,1)}, bf16[2,256,1280]{2,1,0:T(8,128)(2,1)S(1)}, u32[]{:S(2)}) copy-start(bf16[2,256,1280]{2,1,0:T(8,128)(2,1)S(1)} %get-tuple-element.14) | copy-start | bytes 3932164
  7.7 5.2 %copy-start.9 = (bf16[12,4,2048]{2,1,0:T(4,128)(2,1)S(1)}, bf16[12,4,2048]{2,1,0:T(4,128)(2,1)}, u32[]{:S(2)}) copy-start(bf16[12,4,2048]{2,1,0:T(4,128)(2,1)} %param.12) | copy-start | bytes 589828
  7.7 5.5 %copy-start.10 = (f32[1024]{0:T(1024)S(1)}, f32[1024]{0:T(1024)}, u32[]{:S(2)}) copy-start(f32[1024]{0:T(1024)} %param.17) | copy-start | bytes 12292
  7.7 7.6 %copy-start.6 = (s32[3]{0:T(128)S(1)}, s32[3]{0:T(128)}, u32[]{:S(2)}) copy-start(s32[3]{0:T(128)} %len_ref.1) | copy-start | bytes 40
  8.2 16.2 %copy-start.8 = (bf16[2,256,1280]{2,1,0:T(8,128)(2,1)S(1)}, bf16[2,256,1280]{2,1,0:T(8,128)(2,1)}, u32[]{:S(2)}) copy-start(bf16[2,256,1280]{2,1,0:T(8,128)(2,1)} %copy-done.7) | copy-start | bytes 3932164
  8.2 8.8 %collective-permute-start.2 = (bf16[48,512]{1,0:T(8,128)(2,1)S(1)}, bf16[48,512]{1,0:T(8,128)(2,1)S(1)}, u32[]{:S(2)}, u32[]{:S(2)}) collective-permute-start(bf16[48,512]{1,0:T(8,128)(2,1)S(1)} %bitcast.173), channel_id=1, source_target_pairs={{0,2},{1,3},{2,0},{3,1},{4,6},{5,7},{6,4},{7,5},{8,10},{9,11},{10,... | collective-permute-start | bytes 147464 | tf_op jit(solution)/shard_map/ppermute | solution.py:270
  11.2 5.8 %collective-permute-start.3 = (bf16[48,512]{1,0:T(8,128)(2,1)S(1)}, bf16[48,512]{1,0:T(8,128)(2,1)S(1)}, u32[]{:S(2)}, u32[]{:S(2)}) collective-permute-start(bf16[48,512]{1,0:T(8,128)(2,1)S(1)} %bitcast.177), channel_id=1, source_target_pairs={{0,6},{1,7},{2,4},{3,5},{4,2},{5,3},{6,0},{7,1},{8,14},{9,15},{10,... | collective-permute-start | bytes 147464 | tf_op jit(solution)/shard_map/ppermute | solution.py:270
  12.8 4.2 %collective-permute-start.1 = (bf16[48,512]{1,0:T(8,128)(2,1)S(1)}, bf16[48,512]{1,0:T(8,128)(2,1)S(1)}, u32[]{:S(2)}, u32[]{:S(2)}) collective-permute-start(bf16[48,512]{1,0:T(8,128)(2,1)S(1)} %bitcast.175), channel_id=1, source_target_pairs={{0,4},{1,5},{2,6},{3,7},{4,0},{5,1},{6,2},{7,3},{8,12},{9,13},{10,... | collective-permute-start | bytes 147464 | tf_op jit(solution)/shard_map/ppermute | solution.py:270
  13.2 3.7 %collective-permute-start.15 = (f32[1328]{0:T(1024)S(1)}, f32[1328]{0:T(1024)S(1)}, u32[]{:S(2)}, u32[]{:S(2)}) collective-permute-start(f32[1328]{0:T(1024)S(1)} %pad_maximum_fusion.6), channel_id=1, source_target_pairs={{0,2},{1,3},{2,0},{3,1},{4,6},{5,7},{6,4},{7,5},{8,10},{9,11},{10,... | collective-permute-start | bytes 15944 | tf_op jit(solution)/shard_map/ppermute | solution.py:270
  17.2 6.5 %collective-permute-start.4 = (bf16[2,48,512]{2,1,0:T(8,128)(2,1)S(1)}, bf16[2,48,512]{2,1,0:T(8,128)(2,1)S(1)}, u32[]{:S(2)}, u32[]{:S(2)}) collective-permute-start(bf16[2,48,512]{2,1,0:T(8,128)(2,1)S(1)} %get-tuple-element.36), channel_id=1, source_target_pairs={{0,16},{1,17},{2,18},{3,19},{4,20},{5,21},{6,22},{7,23},{8,24},{9,... | collective-permute-start | bytes 294920 | tf_op jit(solution)/shard_map/ppermute | solution.py:270
  23.7 1.7 %collective-permute-start.5 = (bf16[2,2,48,512]{3,2,1,0:T(8,128)(2,1)S(1)}, bf16[2,2,48,512]{3,2,1,0:T(8,128)(2,1)}, u32[]{:S(2)}, u32[]{:S(2)}) collective-permute-start(bf16[2,2,48,512]{3,2,1,0:T(8,128)(2,1)S(1)} %get-tuple-element.33), channel_id=1, source_target_pairs={{0,1},{1,0},{2,3},{3,2},{4,5},{5,4},{6,7},{7,6},{8,9},{9,8},{10,11... | collective-permute-start | bytes 589832 | tf_op jit(solution)/shard_map/ppermute | solution.py:270
  23.9 1.4 %collective-permute-start.16 = (f32[2608]{0:T(1024)S(1)}, f32[2608]{0:T(1024)S(1)}, u32[]{:S(2)}, u32[]{:S(2)}) collective-permute-start(f32[2608]{0:T(1024)S(1)} %pad_maximum_fusion.4), channel_id=1, source_target_pairs={{0,1},{1,0},{2,3},{3,2},{4,5},{5,4},{6,7},{7,6},{8,9},{9,8},{10,11... | collective-permute-start | bytes 31304 | tf_op jit(solution)/shard_map/ppermute | solution.py:270
  24.4 7.0 %collective-permute-start.6 = (bf16[2,256,1280]{2,1,0:T(8,128)(2,1)S(1)}, bf16[2,256,1280]{2,1,0:T(8,128)(2,1)}, u32[]{:S(2)}, u32[]{:S(2)}) collective-permute-start(bf16[2,256,1280]{2,1,0:T(8,128)(2,1)S(1)} %copy-done.8), channel_id=1, source_target_pairs={{0,1},{1,0},{2,3},{3,2},{4,5},{5,4},{6,7},{7,6},{8,9},{9,8},{10,11... | collective-permute-start | bytes 3932168 | tf_op jit(solution)/shard_map/ppermute | solution.py:270
  32.8 13.7 %collective-permute-start.7 = (bf16[2,2,2,24,1280]{4,3,2,1,0:T(8,128)(2,1)S(1)}, bf16[2,2,2,24,1280]{4,3,2,1,0:T(8,128)(2,1)S(1)}, u32[]{:S(2)}, u32[]{:S(2)}) collective-permute-start(bf16[2,2,2,24,1280]{4,3,2,1,0:T(8,128)(2,1)S(1)} %fusion.3), channel_id=1, source_target_pairs={{0,2},{1,3},{2,0},{3,1},{4,6},{5,7},{6,4},{7,5},{8,10},{9,11},{10,... | collective-permute-start | bytes 1474568 | tf_op jit(solution)/shard_map/ppermute | solution.py:270
  37.1 13.1 %collective-permute-start.9 = (bf16[2,2,1,48,1280]{4,3,1,0,2:T(8,128)(2,1)S(1)}, bf16[2,2,1,48,1280]{4,3,1,0,2:T(8,128)(2,1)S(1)}, u32[]{:S(2)}, u32[]{:S(2)}) collective-permute-start(bf16[2,2,1,48,1280]{4,3,1,0,2:T(8,128)(2,1)S(1)} %fusion.5), channel_id=1, source_target_pairs={{0,4},{1,5},{2,6},{3,7},{4,0},{5,1},{6,2},{7,3},{8,12},{9,13},{10,... | collective-permute-start | bytes 1474568 | tf_op jit(solution)/shard_map/ppermute | solution.py:270
  47.9 7.5 %collective-permute-start.8 = (bf16[2,2,24,1280]{3,2,1,0:T(8,128)(2,1)S(1)}, bf16[2,2,24,1280]{3,2,1,0:T(8,128)(2,1)S(1)}, u32[]{:S(2)}, u32[]{:S(2)}) collective-permute-start(bf16[2,2,24,1280]{3,2,1,0:T(8,128)(2,1)S(1)} %fusion.28), channel_id=1, source_target_pairs={{0,4},{1,5},{2,6},{3,7},{4,0},{5,1},{6,2},{7,3},{8,12},{9,13},{10,... | collective-permute-start | bytes 737288 | tf_op jit(solution)/shard_map/ppermute | solution.py:270
  51.6 6.9 %collective-permute-start.10 = (bf16[2,2,24,1280]{3,2,1,0:T(8,128)(2,1)S(1)}, bf16[2,2,24,1280]{3,2,1,0:T(8,128)(2,1)S(1)}, u32[]{:S(2)}, u32[]{:S(2)}) collective-permute-start(bf16[2,2,24,1280]{3,2,1,0:T(8,128)(2,1)S(1)} %fusion.27), channel_id=1, source_target_pairs={{0,2},{1,3},{2,0},{3,1},{4,6},{5,7},{6,4},{7,5},{8,10},{9,11},{10,... | collective-permute-start | bytes 737288 | tf_op jit(solution)/shard_map/ppermute | solution.py:270
  58.5 15.1 %copy-start.2 = (bf16[16,4,128,128]{3,2,1,0:T(8,128)(2,1)S(1)}, bf16[16,4,128,128]{3,2,1,0:T(8,128)(2,1)}, u32[]{:S(2)}) copy-start(bf16[16,4,128,128]{3,2,1,0:T(8,128)(2,1)} %vals.1) | copy-start | bytes 6291460
  58.6 6.0 %collective-permute-start.11 = (bf16[2,24,1280]{2,1,0:T(8,128)(2,1)S(1)}, bf16[2,24,1280]{2,1,0:T(8,128)(2,1)S(1)}, u32[]{:S(2)}, u32[]{:S(2)}) collective-permute-start(bf16[2,24,1280]{2,1,0:T(8,128)(2,1)S(1)} %fusion.32), channel_id=1, source_target_pairs={{0,8},{1,9},{2,10},{3,11},{4,12},{5,13},{6,14},{7,15},{8,0},{9,1},... | collective-permute-start | bytes 368648 | tf_op jit(solution)/shard_map/ppermute | solution.py:270
  60.5 13.1 %copy-start.1 = (bf16[16,4,128,128]{3,2,1,0:T(8,128)(2,1)S(1)}, bf16[16,4,128,128]{3,2,1,0:T(8,128)(2,1)}, u32[]{:S(2)}) copy-start(bf16[16,4,128,128]{3,2,1,0:T(8,128)(2,1)} %keys.1) | copy-start | bytes 6291460
  60.5 13.1 %copy-start.5 = (s32[3,8]{1,0:T(4,128)S(1)}, s32[3,8]{1,0:T(4,128)}, u32[]{:S(2)}) copy-start(s32[3,8]{1,0:T(4,128)} %tab_ref.1) | copy-start | bytes 292
  60.5 11.3 %collective-permute-start.12 = (bf16[2,24,1280]{2,1,0:T(8,128)(2,1)S(1)}, bf16[2,24,1280]{2,1,0:T(8,128)(2,1)S(1)}, u32[]{:S(2)}, u32[]{:S(2)}) collective-permute-start(bf16[2,24,1280]{2,1,0:T(8,128)(2,1)S(1)} %get-tuple-element.17), channel_id=1, source_target_pairs={{0,16},{1,17},{2,18},{3,19},{4,20},{5,21},{6,22},{7,23},{8,24},{9,... | collective-permute-start | bytes 368648 | tf_op jit(solution)/shard_map/ppermute | solution.py:270
  63.9 7.9 %collective-permute-start.13 = (bf16[2,24,1280]{2,1,0:T(8,128)(2,1)S(1)}, bf16[2,24,1280]{2,1,0:T(8,128)(2,1)S(1)}, u32[]{:S(2)}, u32[]{:S(2)}) collective-permute-start(bf16[2,24,1280]{2,1,0:T(8,128)(2,1)S(1)} %get-tuple-element.18), channel_id=1, source_target_pairs={{0,24},{1,25},{2,26},{3,27},{4,28},{5,29},{6,30},{7,31},{8,16},{9,... | collective-permute-start | bytes 368648 | tf_op jit(solution)/shard_map/ppermute | solution.py:270
  72.1 1.5 %collective-permute-start.14 = (f32[2,12,1280]{2,1,0:T(8,128)S(1)}, f32[2,12,1280]{2,1,0:T(8,128)S(1)}, u32[]{:S(2)}, u32[]{:S(2)}) collective-permute-start(f32[2,12,1280]{2,1,0:T(8,128)S(1)} %bitcast.171), channel_id=1, source_target_pairs={{0,1},{1,0},{2,3},{3,2},{4,5},{5,4},{6,7},{7,6},{8,9},{9,8},{10,11... | collective-permute-start | bytes 368648 | tf_op jit(solution)/shard_map/ppermute | solution.py:270
